TPU v7x, 512 devices: a whole 4x4x16 slice. The times are simulated.
512 devices in a mesh: tok: 128 (over y, z, core), head: 4 (over x).
Axes of the slice: x: 4, y: 4, z: 16, core: 2. Of those that a mesh axis runs over, the one named last changes fastest.
Arguments:
- queries: bfloat16 [4, 32768, 256], P('head', 'tok'), may hold values from -5 to 5
- key_vectors: bfloat16 [4, 32768, 256], P('head', 'tok'), may hold values from -5 to 5
- value_vectors: bfloat16 [4, 32768, 256], P('head', 'tok'), may hold values from -8 to 8
- token_rate: float32 [4, 32768], P('head', 'tok'), may hold values from 0.1 to 1
- fast_gate: bfloat16 [4, 512, 256], P('head'), may hold values from -0.375 to 0.375
- fast_up: bfloat16 [4, 512, 256], P('head'), may hold values from -0.375 to 0.375
- fast_down: bfloat16 [4, 512, 256], P('head'), may hold values from -0.25 to 0.25
- attention_gain: float32 [4, 256], P('head'), may hold values from 0.25 to 1.75
- memory_gain: float32 [4, 256], P('head'), may hold values from 0.25 to 1.75
Outputs:
- layer_output: bfloat16 [4, 32768, 256], P('head', 'tok')
All inputs are finite; a program needn't handle non-finite values.
Results may differ from a plain program's by a relative error of at most 0.0065.
Values may be sent and summed in bfloat16 or wider, within the bound.
No kernel may reach another device: no remote copies, remote signals or barrier semaphores. Data moves between devices by JAX's collectives and lax.ppermute only.
A program may use at most 64 MiB of HBM per device.

v0:
```python
import jax
import jax.numpy as jnp
from jax import lax
from jax.sharding import Mesh
from jax.sharding import PartitionSpec as P

BLOCK = 256
HALO = 128
NS_STEPS = 2
TOK = ("tok_0", "tok_1", "tok_2")


first_coeff = 3.4445
second_coeff = -4.775
third_coefficient = 2.0315
step_size = 1.0
norm_floor = 1e-07
epsilon = 1e-06
masked_score = -1e30


def extended(cells, sides, width):
    for axis, dim in sides:
        count = lax.axis_size(axis)
        ends = count - 1
        head = lax.slice_in_dim(cells, 0, width, axis=dim)
        tail = lax.slice_in_dim(cells, cells.shape[dim] - width, cells.shape[dim], axis=dim)
        cells = jnp.concatenate(
            [
                lax.ppermute(tail, axis, [(i, (i + 1) % count) for i in range(ends)]),
                cells,
                lax.ppermute(head, axis, [((i + 1) % count, i) for i in range(ends)]),
            ],
            axis=dim,
        )
    return cells


def from_everyone(array, axis):
    copies = jnp.broadcast_to(array, (lax.axis_size(axis), *array.shape))
    return lax.all_to_all(copies, axis, split_axis=0, concat_axis=0, tiled=True)


def of_everyone(array, axis):
    everything = from_everyone(array, axis)
    return jnp.sum(everything, axis=0)


def split_up(array, dim, peers):
    before, after = (array.shape[:dim], array.shape[dim + 1 :])
    return jnp.moveaxis(array.reshape(*before, peers, -1, *after), dim, 0)


def sum_at_owner(array, axis, dim):
    tiles = split_up(array, dim, lax.axis_size(axis))
    arrived = lax.all_to_all(tiles, axis, split_axis=0, concat_axis=0, tiled=True)
    return arrived.sum(axis=0)


def sum_by_axis(array, axes, dim):
    far, near = axes
    tiles = split_up(array, dim, lax.axis_size(far))
    nearer = sum_at_owner(tiles, near, dim + 1)
    arrived = lax.all_to_all(nearer, far, split_axis=0, concat_axis=0, tiled=True)
    return arrived.sum(axis=0)


def rows_for(lines, peers):
    spare = -lines.shape[0] % peers
    if not spare:
        return lines
    return jnp.concatenate([lines, jnp.zeros((spare, *lines.shape[1:]), lines.dtype)])


def laid_out(tiles, dim):
    tiles = jnp.moveaxis(tiles, 0, dim)
    dims = tiles.shape
    return tiles.reshape(*dims[:dim], dims[dim] * dims[dim + 1], *dims[dim + 2 :])


def gathered_by_axis(array, axes, dim):
    far, near = axes
    tiles = from_everyone(from_everyone(array, far), near)
    return laid_out(tiles.swapaxes(0, 1).reshape(-1, *array.shape), dim)


def sum_by_parts(array, axes):
    lines = array.reshape(-1, array.shape[-1])
    own = sum_by_axis(rows_for(lines, lax.axis_size(axes[0]) * lax.axis_size(axes[1])), axes, 0)
    whole = gathered_by_axis(own, axes, 0)
    return whole[: len(lines)].reshape(array.shape)


def window_attention(probe_matrix_lines, padded_keys, padded_values, first_row, total_rows):
    local_segment_count = probe_matrix_lines.shape[0] // BLOCK
    head_depth = probe_matrix_lines.shape[1]
    key_blocks = padded_keys.reshape(local_segment_count + 1, BLOCK, head_depth)
    value_blocks = padded_values.reshape(local_segment_count + 1, BLOCK, head_depth)
    neighbourhood_lookup_vectors = jnp.concatenate([key_blocks[:-1], key_blocks[1:]], axis=1)
    windowed_values = jnp.concatenate([value_blocks[:-1], value_blocks[1:]], axis=1)
    grouped_probe_vectors = probe_matrix_lines.reshape(local_segment_count, BLOCK, head_depth)
    scores = jnp.einsum(
        "cgf,cyf->cgy",
        grouped_probe_vectors,
        neighbourhood_lookup_vectors,
        preferred_element_type=jnp.float32,
    ) * head_depth ** (-0.5)
    positions = (
        first_row
        - HALO
        + jnp.arange(local_segment_count)[:, None] * BLOCK
        + jnp.arange(2 * BLOCK)[None, :]
    )
    inside = (positions >= 0) & (positions < total_rows)
    scores = jnp.where(inside[:, None, :], scores, masked_score)
    highest = jnp.max(scores, axis=2, keepdims=True)
    weights = jnp.exp(scores - highest)
    denominator = jnp.sum(weights, axis=2, keepdims=True)
    attention_probabilities = (weights / denominator).astype(jnp.bfloat16)
    mixed = jnp.einsum(
        "cir,crv->civ", attention_probabilities, windowed_values, preferred_element_type=jnp.float32
    )
    return mixed.reshape(local_segment_count * BLOCK, head_depth)


def fast_signals(key_rows, value_rows, rates, gate_weights, up_weights, down_weights):
    gate_value = jnp.dot(key_rows, gate_weights.T, preferred_element_type=jnp.float32)
    up_value = jnp.dot(key_rows, up_weights.T, preferred_element_type=jnp.float32)
    squashed = jax.nn.sigmoid(gate_value)
    hidden = (gate_value * squashed * up_value).astype(jnp.bfloat16)
    scaled = (rates[:, None] * value_rows.astype(jnp.float32)).astype(jnp.bfloat16)
    reverse_pass = jnp.dot(scaled, down_weights.T, preferred_element_type=jnp.float32)
    gate_grad = (reverse_pass * up_value * squashed * (1.0 + gate_value * (1.0 - squashed))).astype(
        jnp.bfloat16
    )
    up_grad = (reverse_pass * gate_value * squashed).astype(jnp.bfloat16)
    return (hidden, scaled, gate_grad, up_grad)


def orthogonalize_whole(grads):
    squares = jnp.sum(grads * grads, axis=(0, 2))
    scaling_factor = 1.0 / (jnp.sqrt(squares) + norm_floor)
    current = grads * scaling_factor[None, :, None]
    for iteration in range(NS_STEPS):
        product = jnp.einsum("rbd,rbe->bde", current, current, precision=lax.Precision.HIGHEST)
        squared = jnp.einsum("bde,bef->bdf", product, product, precision=lax.Precision.HIGHEST)
        mixer = second_coeff * product + third_coefficient * squared
        current = first_coeff * current + jnp.einsum(
            "rbd,bde->rbe", current, mixer, precision=lax.Precision.HIGHEST
        )
    return current


def on_device(
    queries,
    key_vectors,
    value_vectors,
    token_rate,
    fast_gate,
    fast_up,
    fast_down,
    attention_gain,
    memory_gain,
):
    heads_here, row_count, head_depth = queries.shape
    hidden_units = fast_gate.shape[1]
    matrices = heads_here * 3
    first_row = lax.axis_index(TOK) * row_count
    total_rows = lax.axis_size(TOK) * row_count
    stacked = jnp.stack([key_vectors, value_vectors])
    padded = extended(stacked, ((TOK, 2),), HALO)
    attended = jax.vmap(window_attention, in_axes=(0, 0, 0, None, None))(
        queries, padded[0], padded[1], first_row, total_rows
    )
    partial_squares = jnp.sum(attended * attended, axis=(0, 2))
    overall_breadth = of_everyone(partial_squares, "head")
    width_mean = overall_breadth / (heads_here * lax.axis_size("head") * head_depth)
    attention_part = (
        attended * lax.rsqrt(width_mean + epsilon)[None, :, None] * attention_gain[:, None, :]
    )
    hidden, scaled, gate_grad, up_grad = jax.vmap(fast_signals)(
        key_vectors, value_vectors, token_rate, fast_gate, fast_up, fast_down
    )
    grad_gate = jnp.einsum(
        "hrf,hrd->fhd", gate_grad, key_vectors, preferred_element_type=jnp.float32
    )
    grad_up = jnp.einsum("hrf,hrd->fhd", up_grad, key_vectors, preferred_element_type=jnp.float32)
    grad_down = jnp.einsum("hrf,hrd->fhd", hidden, scaled, preferred_element_type=jnp.float32)
    accumulated_result = sum_by_parts(
        jnp.stack([grad_gate, grad_up, grad_down], axis=2).reshape(
            hidden_units, matrices * head_depth
        ),
        (("tok_0", "tok_1"), "tok_2"),
    )
    update = orthogonalize_whole(accumulated_result.reshape(hidden_units, matrices, head_depth))
    prior = jnp.stack([fast_gate, fast_up, fast_down], axis=2)
    prior = jnp.transpose(prior, (1, 0, 2, 3)).reshape(hidden_units, matrices, head_depth)
    renewed = (prior.astype(jnp.float32) + step_size * update).astype(jnp.bfloat16)
    portion = renewed.reshape(hidden_units, matrices * head_depth)
    weights = portion.reshape(portion.shape[0], heads_here, 3, head_depth)
    gate_value = jnp.einsum(
        "hrd,fhd->hrf", queries, weights[:, :, 0], preferred_element_type=jnp.float32
    )
    up_value = jnp.einsum(
        "hrd,fhd->hrf", queries, weights[:, :, 1], preferred_element_type=jnp.float32
    )
    memory_hidden = (jax.nn.silu(gate_value) * up_value).astype(jnp.bfloat16)
    memory = jnp.einsum(
        "hrf,fhd->hrd", memory_hidden, weights[:, :, 2], preferred_element_type=jnp.float32
    )
    memory_mean = jnp.mean(memory * memory, axis=2, keepdims=True)
    memory_part = memory * lax.rsqrt(memory_mean + epsilon) * memory_gain[:, None, :]
    return (attention_part + memory_part).astype(jnp.bfloat16)


def solution(mesh):
    finer = Mesh(
        mesh.devices.reshape(4, 16, 2, mesh.shape["head"]), ("tok_0", "tok_1", "tok_2", "head")
    )
    return jax.shard_map(
        on_device,
        mesh=finer,
        in_specs=(
            P("head", TOK, None),
            P("head", TOK, None),
            P("head", TOK, None),
            P("head", TOK),
            P("head", None, None),
            P("head", None, None),
            P("head", None, None),
            P("head", None),
            P("head", None),
        ),
        out_specs=P("head", TOK, None),
        check_vma=False,
    )
```

profile of v0, /device:TPU:1, one launch (start us, length us, event | category | flops | bytes accessed | tf_op | source)
XLA Modules:
  0.0 162.2 jit_solution(5320933217478183733)
XLA Ops:
  0.0 1.3 fusion.24
  1.4 1.3 fusion.26
  4.5 1.1 copy.75
  5.6 2.3 %reshape_reshape_reshape.6 = f32[64,2,4,768]{3,2,1,0:T(4,128)} reshape(f32[512,1,3,256]{3,2,0,1:T(4,128)S(1)} %copy.75) | data formatting | bytes 3145728 | tf_op jit(solution)/shard_map/reshape;reshape;reshape | solution.py:51
  7.8 1.5 copy.76
  9.4 11.5 %all_to_all.26 = f32[2,64,4,768]{3,2,1,0:T(4,128)S(1)} all-to-all(f32[2,64,4,768]{3,2,1,0:T(4,128)S(1)} %copy.76), channel_id=1, replica_groups=mesh['tok_0'=4,'tok_1'=16,'tok_2'=2,'head'=4] {'tok_2'}, dimensions={0} | all-to-all | bytes 3145728 | tf_op jit(solution)/shard_map/all_to_all | solution.py:56
  20.8 1.6 reduce_sum.73
  22.4 13.1 %all-to-all-start.2 = ((f32[64,4,768]{2,1,0:T(4,128)}), f32[64,4,768]{2,1,0:T(4,128)S(1)}, u32[]{:S(2)}, u32[]{:S(2)}) async-start(f32[64,4,768]{2,1,0:T(4,128)} %reduce_sum.73), calls=%async_computation.2 | async-start | bytes 1572864 | tf_op jit(solution)/shard_map/all_to_all | solution.py:64
  35.6 3.7 %collective-permute-start = (bf16[2,1,128,256]{3,2,1,0:T(8,128)(2,1)S(1)}, bf16[2,1,128,256]{3,2,1,0:T(8,128)(2,1)S(1)}, u32[]{:S(2)}, u32[]{:S(2)}) collective-permute-start(bf16[2,1,128,256]{3,2,1,0:T(8,128)(2,1)S(1)} %get-tuple-element.11), channel_id=1, source_target_pairs={{0,4},{4,8},{8,12},{12,16},{16,20},{20,24},{24,28},{28,32},{32,36}... | collective-permute-start | bytes 393224 | tf_op jit(solution)/shard_map/ppermute | solution.py:30
  39.3 1.9 %collective-permute-start.1 = (bf16[2,1,128,256]{3,2,1,0:T(8,128)(2,1)S(1)}, bf16[2,1,128,256]{3,2,1,0:T(8,128)(2,1)S(1)}, u32[]{:S(2)}, u32[]{:S(2)}) collective-permute-start(bf16[2,1,128,256]{3,2,1,0:T(8,128)(2,1)S(1)} %get-tuple-element.12), channel_id=1, source_target_pairs={{4,0},{8,4},{12,8},{16,12},{20,16},{24,20},{28,24},{32,28},{36,32}... | collective-permute-start | bytes 393224 | tf_op jit(solution)/shard_map/ppermute | solution.py:32
  41.2 26.7 %collective-permute-done = bf16[2,1,128,256]{3,2,1,0:T(8,128)(2,1)S(1)} collective-permute-done((bf16[2,1,128,256]{3,2,1,0:T(8,128)(2,1)S(1)}, bf16[2,1,128,256]{3,2,1,0:T(8,128)(2,1)S(1)}, u32[]{:S(2)}, u32[]{:S(2)}) %collective-permute-start) | collective-permute-done | bytes 131104 | tf_op jit(solution)/shard_map/ppermute | solution.py:30
  67.9 4.1 %collective-permute-done.1 = bf16[2,1,128,256]{3,2,1,0:T(8,128)(2,1)S(1)} collective-permute-done((bf16[2,1,128,256]{3,2,1,0:T(8,128)(2,1)S(1)}, bf16[2,1,128,256]{3,2,1,0:T(8,128)(2,1)S(1)}, u32[]{:S(2)}, u32[]{:S(2)}) %collective-permute-start.1) | collective-permute-done | bytes 131104 | tf_op jit(solution)/shard_map/ppermute | solution.py:32
  72.6 1.1 multiply_reduce_fusion.2
  73.6 2.1 %all-to-all-done.2 = f32[64,4,768]{2,1,0:T(4,128)S(1)} async-done(((f32[64,4,768]{2,1,0:T(4,128)}), f32[64,4,768]{2,1,0:T(4,128)S(1)}, u32[]{:S(2)}, u32[]{:S(2)}) %all-to-all-start.2) | async-done | bytes 786464 | tf_op jit(solution)/shard_map/all_to_all | solution.py:64
  75.8 0.6 broadcast_in_dim.20
  76.4 4.0 %all-to-all-start = ((f32[4,1,256]{2,1,0:T(1,128)}), f32[4,1,256]{2,1,0:T(1,128)S(1)}, u32[]{:S(2)}, u32[]{:S(2)}) async-start(f32[4,1,256]{2,1,0:T(1,128)} %broadcast_in_dim.20), calls=%async_computation | async-start | bytes 8192 | tf_op jit(solution)/shard_map/all_to_all | solution.py:41
  80.5 4.0 %all-to-all-done = f32[4,1,256]{2,1,0:T(1,128)S(1)} async-done(((f32[4,1,256]{2,1,0:T(1,128)}), f32[4,1,256]{2,1,0:T(1,128)S(1)}, u32[]{:S(2)}, u32[]{:S(2)}) %all-to-all-start) | async-done | bytes 4128 | tf_op jit(solution)/shard_map/all_to_all | solution.py:41
  84.5 1.0 broadcast_in_dim.34
  85.5 12.4 %all-to-all-start.3 = ((f32[64,4,768]{2,1,0:T(4,128)}), f32[64,4,768]{2,1,0:T(4,128)S(1)}, u32[]{:S(2)}, u32[]{:S(2)}) async-start(f32[64,4,768]{2,1,0:T(4,128)} %broadcast_in_dim.34), calls=%async_computation.3 | async-start | bytes 1572864 | tf_op jit(solution)/shard_map/all_to_all | solution.py:41
  98.1 0.9 copy.72
  99.0 0.9 copy.73
  99.9 36.3 %all-to-all-done.3 = f32[64,4,768]{2,1,0:T(4,128)S(1)} async-done(((f32[64,4,768]{2,1,0:T(4,128)}), f32[64,4,768]{2,1,0:T(4,128)S(1)}, u32[]{:S(2)}, u32[]{:S(2)}) %all-to-all-start.3) | async-done | bytes 786464 | tf_op jit(solution)/shard_map/all_to_all | solution.py:41
  136.4 9.8 %all_to_all.27 = f32[2,64,4,768]{3,2,1,0:T(4,128)S(1)} all-to-all(f32[2,64,4,768]{3,2,1,0:T(4,128)S(1)} %broadcast_in_dim.35), channel_id=1, replica_groups=mesh['tok_0'=4,'tok_1'=16,'tok_2'=2,'head'=4] {'tok_2'}, dimensions={0} | all-to-all | bytes 3145728 | tf_op jit(solution)/shard_map/all_to_all | solution.py:41
  146.8 2.2 %reshape_reshape_reshape.7 = f32[512,3,256]{2,1,0:T(4,128)} reshape(f32[64,2,4,768]{3,2,1,0:T(4,128)S(1)} %copy.78) | data formatting | bytes 3145728 | tf_op jit(solution)/shard_map/reshape;reshape;reshape | solution.py:195
  149.0 1.8 %copy.79 = f32[512,3,256]{0,2,1:T(8,128)S(1)} copy(f32[512,3,256]{2,1,0:T(4,128)} %reshape_reshape_reshape.7) | data formatting | bytes 3145728 | tf_op jit(solution)/shard_map/reshape;reshape;reshape | solution.py:195
  150.9 1.8 %fusion.1 = f32[3,256,256]{2,1,0:T(8,128)S(1)} fusion(f32[512,3,256]{0,2,1:T(8,128)S(1)} %copy.79, f32[3]{0:T(128)S(1)} %add_divide_fusion.1), kind=kOutput, calls=%fused_computation.6 | convolution fusion | flops 1208352768 | bytes 2359308 | tf_op jit(solution)/shard_map/rbd,rbe->bde/dot_general | solution.py:145
  152.7 0.9 fusion.6
  153.6 2.0 %bitcast_add_fusion.1 = f32[512,3,256]{0,2,1:T(8,128)S(1)} fusion(f32[3,256,256]{2,1,0:T(8,128)S(1)} %fusion.6, f32[512,3,256]{0,2,1:T(8,128)S(1)} %copy.79, f32[3]{0:T(128)S(1)} %add_divide_fusion.1), kind=kOutput, calls=%fused_computation.4 | convolution fusion | flops 1209532416 | bytes 3932172 | tf_op jit(solution)/shard_map/rbd,bde->rbe/dot_general | solution.py:148
  155.6 1.6 %fusion.60 = f32[3,256,256]{2,1,0:T(8,128)S(1)} fusion(f32[512,3,256]{0,2,1:T(8,128)S(1)} %bitcast_add_fusion.1), kind=kOutput, calls=%fused_computation.92 | convolution fusion | flops 1207959552 | bytes 2359296 | tf_op jit(solution)/shard_map/rbd,rbe->bde/dot_general | solution.py:145
  157.3 0.9 fusion.5
  158.3 1.8 %fusion.4 = bf16[512,1,3,256]{0,3,2,1:T(8,128)(2,1)S(1)} fusion(f32[3,256,256]{2,1,0:T(8,128)S(1)} %fusion.5, f32[512,3,256]{0,2,1:T(8,128)S(1)} %bitcast_add_fusion.1, bf16[1,512,1,256]{1,3,2,0:T(8,128)(2,1)S(1)} %bitcast.143, bf16[1,512,1,256]{1,3,2,0:T(8,128)(2,1)S(1)} %bitcast.142, bf16[1,512,1,256]{1,3,2,0:T(8,128)(2,1)S(1)} %bitcast.141), kind=kOutput, calls=%fused_computation.9 | convolution fusion | flops 1210712064 | bytes 3932160 | tf_op jit(solution)/shard_map/rbd,bde->rbe/dot_general | solution.py:148
  161.5 0.8 copy.88
  (51 shorter events, 4.9 us)
Async XLA Ops:
  0.0 72.1 %copy-start = (bf16[1,256,256]{2,1,0:T(8,128)(2,1)S(1)}, bf16[1,256,256]{2,1,0:T(8,128)(2,1)}, u32[]{:S(2)}) copy-start(bf16[1,256,256]{2,1,0:T(8,128)(2,1)} %param.9) | copy-start | bytes 393220
  0.0 2.6 %copy-start.2 = (bf16[1,256,256]{2,1,0:T(8,128)(2,1)S(1)}, bf16[1,256,256]{2,1,0:T(8,128)(2,1)}, u32[]{:S(2)}) copy-start(bf16[1,256,256]{2,1,0:T(8,128)(2,1)} %param.11) | copy-start | bytes 393220
  0.0 2.7 %copy-start.5 = (bf16[1,512,256]{2,1,0:T(8,128)(2,1)S(1)}, bf16[1,512,256]{2,1,0:T(8,128)(2,1)}, u32[]{:S(2)}) copy-start(bf16[1,512,256]{2,1,0:T(8,128)(2,1)} %param.15) | copy-start | bytes 786436
  0.0 2.7 %copy-start.11 = (f32[1,256]{1,0:T(1,128)S(1)}, f32[1,256]{1,0:T(1,128)}, u32[]{:S(2)}) copy-start(f32[1,256]{1,0:T(1,128)} %param.12) | copy-start | bytes 3076
  2.7 0.9 copy-start.1
  22.4 53.4 %all-to-all-start.2 = ((f32[64,4,768]{2,1,0:T(4,128)}), f32[64,4,768]{2,1,0:T(4,128)S(1)}, u32[]{:S(2)}, u32[]{:S(2)}) async-start(f32[64,4,768]{2,1,0:T(4,128)} %reduce_sum.73), calls=%async_computation.2 | async-start | bytes 1572864 | tf_op jit(solution)/shard_map/all_to_all | solution.py:64
  35.6 32.3 %collective-permute-start = (bf16[2,1,128,256]{3,2,1,0:T(8,128)(2,1)S(1)}, bf16[2,1,128,256]{3,2,1,0:T(8,128)(2,1)S(1)}, u32[]{:S(2)}, u32[]{:S(2)}) collective-permute-start(bf16[2,1,128,256]{3,2,1,0:T(8,128)(2,1)S(1)} %get-tuple-element.11), channel_id=1, source_target_pairs={{0,4},{4,8},{8,12},{12,16},{16,20},{20,24},{24,28},{28,32},{32,36}... | collective-permute-start | bytes 393224 | tf_op jit(solution)/shard_map/ppermute | solution.py:30
  39.3 32.7 %collective-permute-start.1 = (bf16[2,1,128,256]{3,2,1,0:T(8,128)(2,1)S(1)}, bf16[2,1,128,256]{3,2,1,0:T(8,128)(2,1)S(1)}, u32[]{:S(2)}, u32[]{:S(2)}) collective-permute-start(bf16[2,1,128,256]{3,2,1,0:T(8,128)(2,1)S(1)} %get-tuple-element.12), channel_id=1, source_target_pairs={{4,0},{8,4},{12,8},{16,12},{20,16},{24,20},{28,24},{32,28},{36,32}... | collective-permute-start | bytes 393224 | tf_op jit(solution)/shard_map/ppermute | solution.py:32
  76.4 8.1 %all-to-all-start = ((f32[4,1,256]{2,1,0:T(1,128)}), f32[4,1,256]{2,1,0:T(1,128)S(1)}, u32[]{:S(2)}, u32[]{:S(2)}) async-start(f32[4,1,256]{2,1,0:T(1,128)} %broadcast_in_dim.20), calls=%async_computation | async-start | bytes 8192 | tf_op jit(solution)/shard_map/all_to_all | solution.py:41
  80.4 17.6 %copy-start.3 = (bf16[1,512,256]{2,1,0:T(8,128)(2,1)S(1)}, bf16[1,512,256]{2,1,0:T(8,128)(2,1)}, u32[]{:S(2)}) copy-start(bf16[1,512,256]{2,1,0:T(8,128)(2,1)} %param.13) | copy-start | bytes 786436
  80.5 17.6 %copy-start.4 = (bf16[1,512,256]{2,1,0:T(8,128)(2,1)S(1)}, bf16[1,512,256]{2,1,0:T(8,128)(2,1)}, u32[]{:S(2)}) copy-start(bf16[1,512,256]{2,1,0:T(8,128)(2,1)} %param.14) | copy-start | bytes 786436
  85.5 50.6 %all-to-all-start.3 = ((f32[64,4,768]{2,1,0:T(4,128)}), f32[64,4,768]{2,1,0:T(4,128)S(1)}, u32[]{:S(2)}, u32[]{:S(2)}) async-start(f32[64,4,768]{2,1,0:T(4,128)} %broadcast_in_dim.34), calls=%async_computation.3 | async-start | bytes 1572864 | tf_op jit(solution)/shard_map/all_to_all | solution.py:41
  157.3 1.0 copy-start.6
  157.3 1.0 copy-start.7
  160.4 1.0 copy-start.8
  160.4 0.9 copy-start.9
  160.4 0.9 copy-start.10
where the time goes:
time: 163 us; the launch traced here: 162 us
  waiting for transfers between devices  73.2 us (45%)
  starting transfers between devices  35.2 us (22%)
  blocking collectives  21.2 us (13%)
  matrix products  15.2 us (9%)
  local copies, waits for them, and re-layouts  14.3 us (9%)
  other arithmetic  2.71 us (2%)
    all_to_all x2, waiting for transfers between devices, from_everyone(): return lax.all_to_all(copies, axis, split_axis=0, concat_axis=0, tiled=True)  40.3 us
    ppermute x1, waiting for transfers between devices, extended(): lax.ppermute(tail, axis, [(i, (i + 1) % count) for i in range(ends)])  26.7 us
    all_to_all x2, starting transfers between devices, from_everyone(): return lax.all_to_all(copies, axis, split_axis=0, concat_axis=0, tiled=True)  16.4 us
    all_to_all x1, starting transfers between devices, sum_by_axis(): lax.all_to_all(nearer, far, split_axis=0, concat_axis=0, tiled=True)  13.1 us
    all_to_all x1, blocking collectives, sum_at_owner(): lax.all_to_all(tiles, axis, split_axis=0, concat_axis=0, tiled=True)  11.5 us
    all_to_all x1, blocking collectives, from_everyone(): return lax.all_to_all(copies, axis, split_axis=0, concat_axis=0, tiled=True)  9.78 us
    ppermute x1, waiting for transfers between devices, extended(): lax.ppermute(head, axis, [((i + 1) % count, i) for i in range(ends)])  4.11 us
    another operation x2, local copies, waits for them, and re-layouts, on_device(): accumulated_result.reshape(hidden_units, matrices, head_depth)  4.06 us
  transfers between devices with their start and end apart: 5, of which 5 were waited for; matrix products, arithmetic and copies ran while one was open for 2% of the time, Pallas kernels for 0%

commit v1 on v0

v1 whole, which is shorter than its diff:
```python
import jax
import jax.numpy as jnp
from jax import lax
from jax.sharding import Mesh
from jax.sharding import PartitionSpec as P

BLOCK = 256
HALO = 128
NS_STEPS = 2
TOK = ("y", "zh", "zl", "c")
NEAR = ("y", "zl")
FAR = "zh"
PAIR = "c"

first_coeff = 3.4445
second_coeff = -4.775
third_coefficient = 2.0315
step_size = 1.0
norm_floor = 1e-07
epsilon = 1e-06
masked_score = -1e30


def dot(a, b, dims, precision=None):
    return lax.dot_general(
        a, b, (dims, ((), ())), precision=precision, preferred_element_type=jnp.float32
    )


def outer_halo(keys, values, core):
    count = lax.axis_size(TOK)
    swap = [(i, i + 1) for i in range(1, count - 1, 2)] + [(i + 1, i) for i in range(1, count - 1, 2)]
    stacked = jnp.stack([keys, values])
    edge = jnp.where(core == 0, stacked[:, :HALO], stacked[:, -HALO:])
    return lax.ppermute(edge, TOK, swap)


def copies_to(array, axis):
    copies = jnp.broadcast_to(array, (lax.axis_size(axis), *array.shape))
    return lax.all_to_all(copies, axis, split_axis=0, concat_axis=0, tiled=True)


def window_attention(queries, pair_keys, pair_values, outer, core, has_outer):
    head_depth = queries.shape[1]
    start = core * HALO
    width = 2 * BLOCK - HALO
    keys = lax.dynamic_slice_in_dim(pair_keys, start, width, 0)
    values = lax.dynamic_slice_in_dim(pair_values, start, width, 0)
    scale = head_depth ** (-0.5)
    inner = dot(queries, keys, ((1,), (1,))) * scale
    outside = dot(queries, outer[0], ((1,), (1,))) * scale
    outside = jnp.where(has_outer, outside, masked_score)
    highest = jnp.maximum(
        jnp.max(inner, axis=1, keepdims=True), jnp.max(outside, axis=1, keepdims=True)
    )
    inner = jnp.exp(inner - highest)
    outside = jnp.exp(outside - highest)
    total = jnp.sum(inner, axis=1, keepdims=True) + jnp.sum(outside, axis=1, keepdims=True)
    inner = (inner / total).astype(jnp.bfloat16)
    outside = (outside / total).astype(jnp.bfloat16)
    return dot(inner, values, ((1,), (0,))) + dot(outside, outer[1], ((1,), (0,)))


def fast_gradients(keys, scaled, gate_weights, up_weights, down_weights):
    gate_value = dot(keys, gate_weights, ((1,), (1,)))
    up_value = dot(keys, up_weights, ((1,), (1,)))
    squashed = jax.nn.sigmoid(gate_value)
    hidden = (gate_value * squashed * up_value).astype(jnp.bfloat16)
    backward = dot(scaled, down_weights, ((1,), (1,)))
    gate_grad = (backward * up_value * squashed * (1.0 + gate_value * (1.0 - squashed))).astype(
        jnp.bfloat16
    )
    up_grad = (backward * gate_value * squashed).astype(jnp.bfloat16)
    return jnp.concatenate(
        [
            dot(gate_grad, keys, ((0,), (0,))).astype(jnp.bfloat16),
            dot(up_grad, keys, ((0,), (0,))).astype(jnp.bfloat16),
            dot(hidden, scaled, ((0,), (0,))).astype(jnp.bfloat16),
        ],
        axis=1,
    )


def sum_over_tokens(grads):
    near = lax.axis_size(NEAR)
    tiles = grads.reshape(near, -1, grads.shape[1])
    arrived = lax.all_to_all(tiles, NEAR, split_axis=0, concat_axis=0, tiled=True)
    own = jnp.sum(arrived.astype(jnp.float32), axis=0).astype(jnp.bfloat16)
    own = jnp.sum(copies_to(own, FAR).astype(jnp.float32), axis=0).astype(jnp.bfloat16)
    half = copies_to(own, NEAR).reshape(grads.shape)
    return lax.all_gather(half, PAIR, axis=0, tiled=True)


def orthogonalize(grad):
    grad = grad.astype(jnp.float32)
    current = grad * (1.0 / (jnp.sqrt(jnp.sum(grad * grad)) + norm_floor))
    for iteration in range(NS_STEPS):
        product = dot(current, current, ((0,), (0,)), lax.Precision.HIGH)
        squared = dot(product, product, ((1,), (0,)), lax.Precision.HIGH)
        mixer = second_coeff * product + third_coefficient * squared
        current = first_coeff * current + dot(current, mixer, ((1,), (0,)), lax.Precision.HIGH)
    return current


def on_device(
    queries,
    key_vectors,
    value_vectors,
    token_rate,
    fast_gate,
    fast_up,
    fast_down,
    attention_gain,
    memory_gain,
):
    queries, keys, values = queries[0], key_vectors[0], value_vectors[0]
    rates = token_rate[0]
    head_depth = queries.shape[1]
    hidden_units = fast_gate.shape[1]
    core = lax.axis_index(PAIR)
    index = lax.axis_index(TOK)
    has_outer = jnp.where(core == 0, index > 0, index < lax.axis_size(TOK) - 1)

    scaled = (rates[:, None] * values.astype(jnp.float32)).astype(jnp.bfloat16)
    pair = lax.all_gather(jnp.stack([keys, scaled, values]), PAIR, axis=1, tiled=True)
    half = hidden_units // 2
    mine = [
        lax.dynamic_slice_in_dim(w[0], core * half, half, 0) for w in (fast_gate, fast_up, fast_down)
    ]
    grads = fast_gradients(pair[0], pair[1], *mine)
    summed = sum_over_tokens(grads)

    outer = outer_halo(keys, values, core)
    attended = window_attention(queries, pair[0], pair[2], outer, core, has_outer)
    squares = jnp.sum(attended * attended, axis=1)
    width_sum = jnp.sum(copies_to(squares.reshape(1, -1), "head"), axis=0)[0]
    width_mean = width_sum / (lax.axis_size("head") * head_depth)
    attention_part = attended * lax.rsqrt(width_mean + epsilon)[:, None] * attention_gain

    renewed = []
    for i, w in enumerate((fast_gate, fast_up, fast_down)):
        update = orthogonalize(summed[:, i * head_depth : (i + 1) * head_depth])
        renewed.append((w[0].astype(jnp.float32) + step_size * update).astype(jnp.bfloat16))
    gate_value = dot(queries, renewed[0], ((1,), (1,)))
    up_value = dot(queries, renewed[1], ((1,), (1,)))
    memory_hidden = (jax.nn.silu(gate_value) * up_value).astype(jnp.bfloat16)
    memory = dot(memory_hidden, renewed[2], ((1,), (0,)))
    memory_mean = jnp.mean(memory * memory, axis=1, keepdims=True)
    memory_part = memory * lax.rsqrt(memory_mean + epsilon) * memory_gain
    return (attention_part + memory_part).astype(jnp.bfloat16)[None]


def solution(mesh):
    finer = Mesh(
        mesh.devices.reshape(4, 4, 4, 2, mesh.shape["head"]), ("y", "zh", "zl", "c", "head")
    )
    return jax.shard_map(
        on_device,
        mesh=finer,
        in_specs=(
            P("head", TOK, None),
            P("head", TOK, None),
            P("head", TOK, None),
            P("head", TOK),
            P("head", None, None),
            P("head", None, None),
            P("head", None, None),
            P("head", None),
            P("head", None),
        ),
        out_specs=P("head", TOK, None),
        check_vma=False,
    )
```

time: 163 us -> 102 us (0.63)
  waiting for transfers between devices: 73.2 us -> 34 us
  local copies, waits for them, and re-layouts: 14.3 us -> 6.51 us
  starting transfers between devices: 35.2 us -> 27.8 us
  blocking collectives: 21.2 us -> 16.4 us
  matrix products: 15.2 us -> 11.4 us
  between operations: 0.37 us -> 2.55 us
    ppermute x2 -> x1, waiting for transfers between devices: 30.8 us -> 5.51 us  [outer_halo(): return lax.ppermute(edge, TOK, swap)]
    all_to_all x2 -> x0, blocking collectives: 21.2 us -> none  [the longest x1 11.5 us: sum_at_owner(): lax.all_to_all(tiles, axis, split_axis=0, concat_axis=0, tiled=True)]
    all_gather x0 -> x2, blocking collectives: none -> 16.4 us  [the longest x1 8.97 us: on_device(): lax.all_gather(jnp.stack([keys, scaled, values]), PAIR, axis=1, tiled=True)]
    all_to_all x3 -> x4, waiting for transfers between devices: 42.5 us -> 28.5 us  [the longest x3 25.4 us: copies_to(): return lax.all_to_all(copies, axis, split_axis=0, concat_axis=0, tiled=True)]
    another operation x4 -> x1, local copies, waits for them, and re-layouts: 7.42 us -> 0.01 us  [outer_halo(): stacked = jnp.stack([keys, values])]
    all_to_all x3 -> x4, starting transfers between devices: 29.5 us -> 24.1 us  [the longest x3 20.6 us: copies_to(): return lax.all_to_all(copies, axis, split_axis=0, concat_axis=0, tiled=True)]
    dot_general x16 -> x30, matrix products: 15.2 us -> 11.4 us  [dot(): lax.dot_general(a, b, (dims, ((), ())), precision=precision, preferred_el...]
    ppermute x2 -> x1, starting transfers between devices: 5.66 us -> 3.7 us  [outer_halo(): return lax.ppermute(edge, TOK, swap)]
  transfers between devices with their start and end apart: 5 -> 5, of which waited for: 5 -> 5; matrix products, arithmetic and copies ran while one was open for 2% -> 1% of each run, Pallas kernels for 0% -> 0%
where the time goes in v1:
time: 102 us; the launch traced here: 101 us
  waiting for transfers between devices  34 us (33%)
  starting transfers between devices  27.8 us (27%)
  blocking collectives  16.4 us (16%)
  matrix products  11.4 us (11%)
  local copies, waits for them, and re-layouts  6.51 us (6%)
  between operations  2.55 us (2%)
  other arithmetic  2.41 us (2%)
    all_to_all x3, waiting for transfers between devices, copies_to(): return lax.all_to_all(copies, axis, split_axis=0, concat_axis=0, tiled=True)  25.4 us
    all_to_all x3, starting transfers between devices, copies_to(): return lax.all_to_all(copies, axis, split_axis=0, concat_axis=0, tiled=True)  20.6 us
    dot_general x30, matrix products, dot(): lax.dot_general(a, b, (dims, ((), ())), precision=precision, preferred_el...  11.4 us
    all_gather x1, blocking collectives, on_device(): lax.all_gather(jnp.stack([keys, scaled, values]), PAIR, axis=1, tiled=True)  8.97 us
    all_gather x1, blocking collectives, sum_over_tokens(): return lax.all_gather(half, PAIR, axis=0, tiled=True)  7.42 us
    ppermute x1, waiting for transfers between devices, outer_halo(): return lax.ppermute(edge, TOK, swap)  5.51 us
    ppermute x1, starting transfers between devices, outer_halo(): return lax.ppermute(edge, TOK, swap)  3.7 us
    all_to_all x1, starting transfers between devices, sum_over_tokens(): lax.all_to_all(tiles, NEAR, split_axis=0, concat_axis=0, tiled=True)  3.55 us
  transfers between devices with their start and end apart: 5, of which 5 were waited for; matrix products, arithmetic and copies ran while one was open for 1% of the time, Pallas kernels for 0%

profile of v1, /device:TPU:1, one launch (start us, length us, event | category | flops | bytes accessed | tf_op | source)
XLA Modules:
  0.0 101.0 jit_solution(8072750087071840205)
XLA Ops:
  0.0 0.7 copy-done.6
  0.7 1.1 %multiply_convert_fusion.3 = bf16[1,256,256]{2,1,0:T(8,128)(2,1)S(1)} fusion(bf16[1,256,256]{2,1,0:T(8,128)(2,1)} %param.11, f32[256]{0:T(256)S(1)} %bitcast.115), kind=kLoop, calls=%fused_computation.82 | loop fusion | flops 196608 | bytes 263168 | tf_op jit(solution)/shard_map/convert_element_type | solution.py:124
  1.9 9.0 %all_gather.6 = bf16[3,512,256]{2,1,0:T(8,128)(2,1)S(1)} all-gather(bf16[3,256,256]{2,1,0:T(8,128)(2,1)S(1)} %pad_maximum_fusion), channel_id=1, replica_groups=mesh['y'=4,'zh'=4,'zl'=4,'c'=2,'head'=4] {'c'}, dimensions={1}, use_global_device_ids=true | all-gather | bytes 1179648 | tf_op jit(solution)/shard_map/all_gather | solution.py:125
  11.1 0.7 copy-done.3
  12.1 0.7 copy-done.4
  13.4 0.4 convolution_convert_fusion.2
  14.2 0.9 copy.16
  15.2 3.6 %all-to-all-start.1 = ((bf16[16,16,768]{2,1,0:T(8,128)(2,1)}), bf16[16,16,768]{2,1,0:T(8,128)(2,1)S(1)}, u32[]{:S(2)}, u32[]{:S(2)}) async-start(bf16[16,16,768]{2,1,0:T(8,128)(2,1)} %bitcast.13), calls=%async_computation.1 | async-start | bytes 786432 | tf_op jit(solution)/shard_map/all_to_all | solution.py:87
  18.8 3.7 %collective-permute-start = (bf16[2,128,256]{2,1,0:T(8,128)(2,1)S(1)}, bf16[2,128,256]{2,1,0:T(8,128)(2,1)S(1)}, u32[]{:S(2)}, u32[]{:S(2)}) collective-permute-start(bf16[2,128,256]{2,1,0:T(8,128)(2,1)S(1)} %slice_select_fusion), channel_id=1, source_target_pairs={{4,8},{12,16},{20,24},{28,32},{36,40},{44,48},{52,56},{60,64},{68,... | collective-permute-start | bytes 393224 | tf_op jit(solution)/shard_map/ppermute | solution.py:35
  22.8 5.5 %collective-permute-done = bf16[2,128,256]{2,1,0:T(8,128)(2,1)S(1)} collective-permute-done((bf16[2,128,256]{2,1,0:T(8,128)(2,1)S(1)}, bf16[2,128,256]{2,1,0:T(8,128)(2,1)S(1)}, u32[]{:S(2)}, u32[]{:S(2)}) %collective-permute-start) | collective-permute-done | bytes 131104 | tf_op jit(solution)/shard_map/ppermute | solution.py:35
  28.7 3.1 %all-to-all-done.1 = bf16[16,16,768]{2,1,0:T(8,128)(2,1)S(1)} async-done(((bf16[16,16,768]{2,1,0:T(8,128)(2,1)}), bf16[16,16,768]{2,1,0:T(8,128)(2,1)S(1)}, u32[]{:S(2)}, u32[]{:S(2)}) %all-to-all-start.1) | async-done | bytes 393248 | tf_op jit(solution)/shard_map/all_to_all | solution.py:87
  31.8 0.6 broadcast_in_dim.24
  32.5 11.5 %all-to-all-start.2 = ((bf16[4,16,768]{2,1,0:T(8,128)(2,1)}), bf16[4,16,768]{2,1,0:T(8,128)(2,1)S(1)}, u32[]{:S(2)}, u32[]{:S(2)}) async-start(bf16[4,16,768]{2,1,0:T(8,128)(2,1)} %broadcast_in_dim.24), calls=%async_computation.2 | async-start | bytes 196608 | tf_op jit(solution)/shard_map/all_to_all | solution.py:40
  44.5 11.4 %all-to-all-done.2 = bf16[4,16,768]{2,1,0:T(8,128)(2,1)S(1)} async-done(((bf16[4,16,768]{2,1,0:T(8,128)(2,1)}), bf16[4,16,768]{2,1,0:T(8,128)(2,1)S(1)}, u32[]{:S(2)}, u32[]{:S(2)}) %all-to-all-start.2) | async-done | bytes 98336 | tf_op jit(solution)/shard_map/all_to_all | solution.py:40
  55.9 0.6 broadcast_in_dim.23
  56.5 4.0 %all-to-all-start = ((f32[4,1,256]{2,1,0:T(1,128)}), f32[4,1,256]{2,1,0:T(1,128)S(1)}, u32[]{:S(2)}, u32[]{:S(2)}) async-start(f32[4,1,256]{2,1,0:T(1,128)} %broadcast_in_dim.23), calls=%async_computation | async-start | bytes 8192 | tf_op jit(solution)/shard_map/all_to_all | solution.py:40
  60.6 4.1 %all-to-all-done = f32[4,1,256]{2,1,0:T(1,128)S(1)} async-done(((f32[4,1,256]{2,1,0:T(1,128)}), f32[4,1,256]{2,1,0:T(1,128)S(1)}, u32[]{:S(2)}, u32[]{:S(2)}) %all-to-all-start) | async-done | bytes 4128 | tf_op jit(solution)/shard_map/all_to_all | solution.py:40
  64.7 0.8 broadcast_in_dim.25
  65.4 5.1 %all-to-all-start.3 = ((bf16[16,16,768]{2,1,0:T(8,128)(2,1)}), bf16[16,16,768]{2,1,0:T(8,128)(2,1)S(1)}, u32[]{:S(2)}, u32[]{:S(2)}) async-start(bf16[16,16,768]{2,1,0:T(8,128)(2,1)} %broadcast_in_dim.25), calls=%async_computation.3 | async-start | bytes 786432 | tf_op jit(solution)/shard_map/all_to_all | solution.py:40
  70.6 9.9 %all-to-all-done.3 = bf16[16,16,768]{2,1,0:T(8,128)(2,1)S(1)} async-done(((bf16[16,16,768]{2,1,0:T(8,128)(2,1)}), bf16[16,16,768]{2,1,0:T(8,128)(2,1)S(1)}, u32[]{:S(2)}, u32[]{:S(2)}) %all-to-all-start.3) | async-done | bytes 393248 | tf_op jit(solution)/shard_map/all_to_all | solution.py:40
  80.5 7.4 %all_gather.7 = bf16[512,768]{1,0:T(8,128)(2,1)S(1)} all-gather(bf16[256,768]{1,0:T(8,128)(2,1)S(1)} %bitcast.114), channel_id=1, replica_groups=mesh['y'=4,'zh'=4,'zl'=4,'c'=2,'head'=4] {'c'}, dimensions={0}, use_global_device_ids=true | all-gather | bytes 1179648 | tf_op jit(solution)/shard_map/all_gather | solution.py:91
  87.9 0.8 fusion.22
  89.5 0.6 fusion.20
  90.7 0.6 fusion.90
  91.6 0.4 fusion.4
  93.0 0.6 fusion.18
  94.2 0.6 fusion.91
  96.3 0.6 fusion.16
  97.6 0.6 fusion.92
  98.9 0.5 multiply_reduce_fusion
  99.6 0.5 copy-done.7
  100.2 0.8 copy.17
  (51 shorter events, 7.1 us)
Async XLA Ops:
  0.0 22.6 %copy-start = (bf16[1,256,256]{2,1,0:T(8,128)(2,1)S(1)}, bf16[1,256,256]{2,1,0:T(8,128)(2,1)}, u32[]{:S(2)}) copy-start(bf16[1,256,256]{2,1,0:T(8,128)(2,1)} %param.9) | copy-start | bytes 393220
  0.0 0.7 copy-start.6
  0.7 1.1 %copy-start.1 = (bf16[1,256,256]{2,1,0:T(8,128)(2,1)S(1)}, bf16[1,256,256]{2,1,0:T(8,128)(2,1)}, u32[]{:S(2)}) copy-start(bf16[1,256,256]{2,1,0:T(8,128)(2,1)} %param.11) | copy-start | bytes 393220
  0.7 1.1 %copy-start.5 = (bf16[1,256,256]{2,1,0:T(8,128)(2,1)S(1)}, bf16[1,256,256]{2,1,0:T(8,128)(2,1)}, u32[]{:S(2)}) copy-start(bf16[1,256,256]{2,1,0:T(8,128)(2,1)} %param.10) | copy-start | bytes 393220
  1.9 9.0 %copy-start.2 = (bf16[1,512,256]{2,1,0:T(8,128)(2,1)S(1)}, bf16[1,512,256]{2,1,0:T(8,128)(2,1)}, u32[]{:S(2)}) copy-start(bf16[1,512,256]{2,1,0:T(8,128)(2,1)} %param.13) | copy-start | bytes 786436
  10.9 1.0 copy-start.3
  11.8 0.9 copy-start.4
  15.2 16.6 %all-to-all-start.1 = ((bf16[16,16,768]{2,1,0:T(8,128)(2,1)}), bf16[16,16,768]{2,1,0:T(8,128)(2,1)S(1)}, u32[]{:S(2)}, u32[]{:S(2)}) async-start(bf16[16,16,768]{2,1,0:T(8,128)(2,1)} %bitcast.13), calls=%async_computation.1 | async-start | bytes 786432 | tf_op jit(solution)/shard_map/all_to_all | solution.py:87
  18.8 9.6 %collective-permute-start = (bf16[2,128,256]{2,1,0:T(8,128)(2,1)S(1)}, bf16[2,128,256]{2,1,0:T(8,128)(2,1)S(1)}, u32[]{:S(2)}, u32[]{:S(2)}) collective-permute-start(bf16[2,128,256]{2,1,0:T(8,128)(2,1)S(1)} %slice_select_fusion), channel_id=1, source_target_pairs={{4,8},{12,16},{20,24},{28,32},{36,40},{44,48},{52,56},{60,64},{68,... | collective-permute-start | bytes 393224 | tf_op jit(solution)/shard_map/ppermute | solution.py:35
  32.5 23.4 %all-to-all-start.2 = ((bf16[4,16,768]{2,1,0:T(8,128)(2,1)}), bf16[4,16,768]{2,1,0:T(8,128)(2,1)S(1)}, u32[]{:S(2)}, u32[]{:S(2)}) async-start(bf16[4,16,768]{2,1,0:T(8,128)(2,1)} %broadcast_in_dim.24), calls=%async_computation.2 | async-start | bytes 196608 | tf_op jit(solution)/shard_map/all_to_all | solution.py:40
  56.5 8.2 %all-to-all-start = ((f32[4,1,256]{2,1,0:T(1,128)}), f32[4,1,256]{2,1,0:T(1,128)S(1)}, u32[]{:S(2)}, u32[]{:S(2)}) async-start(f32[4,1,256]{2,1,0:T(1,128)} %broadcast_in_dim.23), calls=%async_computation | async-start | bytes 8192 | tf_op jit(solution)/shard_map/all_to_all | solution.py:40
  65.4 15.0 %all-to-all-start.3 = ((bf16[16,16,768]{2,1,0:T(8,128)(2,1)}), bf16[16,16,768]{2,1,0:T(8,128)(2,1)S(1)}, u32[]{:S(2)}, u32[]{:S(2)}) async-start(bf16[16,16,768]{2,1,0:T(8,128)(2,1)} %broadcast_in_dim.25), calls=%async_computation.3 | async-start | bytes 786432 | tf_op jit(solution)/shard_map/all_to_all | solution.py:40
  98.9 0.7 copy-start.8
  99.4 0.7 copy-start.7

commit v2 on v1

v2 whole, which is shorter than its diff:
```python
import functools

import jax
import jax.numpy as jnp
from jax import lax
from jax.experimental import pallas as pl
from jax.experimental.pallas import tpu as pltpu
from jax.sharding import Mesh
from jax.sharding import PartitionSpec as P


HALO = 128
NS_STEPS = 2
TOK = ("y", "zh", "zl", "c")
NEAR = ("y", "zl")
FAR = "zh"
PAIR = "c"

first_coeff = 3.4445
second_coeff = -4.775
third_coefficient = 2.0315
step_size = 1.0
norm_floor = 1e-07
epsilon = 1e-06
masked_score = -1e30

VMEM = pl.BlockSpec(memory_space=pltpu.VMEM)
SMEM = pl.BlockSpec(memory_space=pltpu.SMEM)


def dot(a, b, dims):
    return lax.dot_general(a, b, (dims, ((), ())), preferred_element_type=jnp.float32)


def outer_halo(keys, values, core):
    count = lax.axis_size(TOK)
    ends = range(1, count - 1, 2)
    swap = [(i, i + 1) for i in ends] + [(i + 1, i) for i in ends]
    first = jnp.stack([keys[:HALO], values[:HALO]])
    last = jnp.stack([keys[-HALO:], values[-HALO:]])
    return lax.ppermute(jnp.where(core == 0, first, last), TOK, swap)


def from_partner(array):
    return lax.ppermute(array, PAIR, [(0, 1), (1, 0)])


def exchange(tiles, axis):
    return lax.all_to_all(tiles, axis, split_axis=0, concat_axis=0, tiled=True)


def copies_to(array, axis):
    copies = jnp.broadcast_to(array, (lax.axis_size(axis), *array.shape))
    return exchange(copies, axis)


def head_sum(partial):
    heads = lax.axis_size("head")
    distance = 1
    while distance < heads:
        pairs = [(i, i ^ distance) for i in range(heads)]
        partial = partial + lax.ppermute(partial, "head", pairs)
        distance *= 2
    return partial


def window_attention(queries, keys, values, partner_keys, partner_values, outer, core, has_outer):
    head_depth = queries.shape[1]
    near_keys = lax.dynamic_slice_in_dim(partner_keys, core * HALO, HALO, 0)
    near_values = lax.dynamic_slice_in_dim(partner_values, core * HALO, HALO, 0)
    scale = head_depth ** (-0.5)
    scores = [dot(queries, k, ((1,), (1,))) * scale for k in (keys, near_keys, outer[0])]
    scores[2] = jnp.where(has_outer, scores[2], masked_score)
    highest = functools.reduce(jnp.maximum, [jnp.max(s, axis=1, keepdims=True) for s in scores])
    weights = [jnp.exp(s - highest) for s in scores]
    total = sum(jnp.sum(w, axis=1, keepdims=True) for w in weights)
    parts = [
        dot((w / total).astype(jnp.bfloat16), v, ((1,), (0,)))
        for w, v in zip(weights, (values, near_values, outer[1]))
    ]
    return parts[0] + parts[1] + parts[2]


def gradient_kernel(core_ref, own_ref, partner_ref, gate_ref, up_ref, down_ref, out_ref):
    half = out_ref.shape[0]
    depth = gate_ref.shape[2]
    mine = pl.ds(pl.multiple_of(core_ref[0] * half, half), half)
    gate_weights, up_weights, down_weights = gate_ref[0, mine], up_ref[0, mine], down_ref[0, mine]
    sums = [0.0, 0.0, 0.0]
    for ref in (own_ref, partner_ref):
        keys, scaled = ref[0], ref[1]
        gate_value = dot(keys, gate_weights, ((1,), (1,)))
        up_value = dot(keys, up_weights, ((1,), (1,)))
        backward = dot(scaled, down_weights, ((1,), (1,)))
        squashed = jax.nn.sigmoid(gate_value)
        silu = gate_value * squashed
        hidden = (silu * up_value).astype(jnp.bfloat16)
        gate_grad = (
            backward * up_value * squashed * (1.0 + gate_value * (1.0 - squashed))
        ).astype(jnp.bfloat16)
        up_grad = (backward * silu).astype(jnp.bfloat16)
        sums[0] += dot(gate_grad, keys, ((0,), (0,)))
        sums[1] += dot(up_grad, keys, ((0,), (0,)))
        sums[2] += dot(hidden, scaled, ((0,), (0,)))
    for i, total in enumerate(sums):
        out_ref[:, i * depth : (i + 1) * depth] = total.astype(jnp.bfloat16)


def renew_kernel(
    core_ref,
    own_ref,
    partner_ref,
    gate_ref,
    up_ref,
    down_ref,
    queries_ref,
    attention_ref,
    gain_ref,
    out_ref,
):
    half = own_ref.shape[0]
    depth = gate_ref.shape[2]
    core = core_ref[0]
    rows = [pl.ds(pl.multiple_of(c * half, half), half) for c in (core, 1 - core)]
    renewed = []
    for i, weights_ref in enumerate((gate_ref, up_ref, down_ref)):
        grads = [ref[:, i * depth : (i + 1) * depth] for ref in (own_ref, partner_ref)]
        wide = [g.astype(jnp.float32) for g in grads]
        squares = jnp.sum(wide[0] * wide[0] + wide[1] * wide[1], axis=0, keepdims=True)
        norm = jnp.sqrt(jnp.sum(squares, axis=1, keepdims=True))
        scaling = 1.0 / (norm + norm_floor)
        current = [g * scaling for g in wide]
        for _ in range(NS_STEPS):
            rounded = [c.astype(jnp.bfloat16) for c in current]
            product = sum(dot(c, c, ((0,), (0,))) for c in rounded)
            low = product.astype(jnp.bfloat16)
            squared = dot(low, low, ((1,), (0,)))
            mixer = (second_coeff * product + third_coefficient * squared).astype(jnp.bfloat16)
            current = [
                first_coeff * c + dot(r, mixer, ((1,), (0,))) for c, r in zip(current, rounded)
            ]
        renewed.append(
            [
                (weights_ref[0, r].astype(jnp.float32) + step_size * c).astype(jnp.bfloat16)
                for r, c in zip(rows, current)
            ]
        )
    queries = queries_ref[0]
    memory = 0.0
    for gate_weights, up_weights, down_weights in zip(*renewed):
        gate_value = dot(queries, gate_weights, ((1,), (1,)))
        up_value = dot(queries, up_weights, ((1,), (1,)))
        hidden = (gate_value * jax.nn.sigmoid(gate_value) * up_value).astype(jnp.bfloat16)
        memory += dot(hidden, down_weights, ((1,), (0,)))
    mean = jnp.mean(memory * memory, axis=1, keepdims=True)
    memory_part = memory * lax.rsqrt(mean + epsilon) * gain_ref[...]
    out_ref[0] = (attention_ref[...] + memory_part).astype(jnp.bfloat16)


def call(kernel, shape, flops, *args):
    return pl.pallas_call(
        kernel,
        out_shape=jax.ShapeDtypeStruct(shape, jnp.bfloat16),
        in_specs=[SMEM] + [VMEM] * (len(args) - 1),
        out_specs=VMEM,
        compiler_params=pltpu.CompilerParams(vmem_limit_bytes=32 * 2**20),
        cost_estimate=pl.CostEstimate(
            flops=flops, bytes_accessed=2**20, transcendentals=2**17
        ),
    )(*args)


def on_device(
    queries,
    key_vectors,
    value_vectors,
    token_rate,
    fast_gate,
    fast_up,
    fast_down,
    attention_gain,
    memory_gain,
):
    keys, values = key_vectors[0], value_vectors[0]
    head_depth = keys.shape[1]
    hidden_units = fast_gate.shape[1]
    core = lax.axis_index(PAIR)
    core_vector = core.reshape(1)
    index = lax.axis_index(TOK)
    has_outer = jnp.where(core == 0, index > 0, index < lax.axis_size(TOK) - 1)

    scaled = (token_rate[0][:, None] * values.astype(jnp.float32)).astype(jnp.bfloat16)
    own = jnp.stack([keys, scaled, values])
    partner = from_partner(own)
    half = hidden_units // 2
    grads = call(
        gradient_kernel,
        (half, 3 * head_depth),
        2**30,
        core_vector,
        own,
        partner,
        fast_gate,
        fast_up,
        fast_down,
    )
    near = lax.axis_size(NEAR)
    tiles = grads.reshape(near, half // near, 3 * head_depth)
    arrived = exchange(tiles, NEAR)
    sums = jnp.sum(arrived.astype(jnp.float32), axis=0).astype(jnp.bfloat16)
    sums = jnp.sum(copies_to(sums, FAR).astype(jnp.float32), axis=0).astype(jnp.bfloat16)
    own_sum = copies_to(sums, NEAR).reshape(half, 3 * head_depth)
    partner_sum = from_partner(own_sum)

    outer = outer_halo(keys, values, core)
    attended = window_attention(
        queries[0], keys, values, partner[0], partner[2], outer, core, has_outer
    )
    squares = jnp.sum(attended * attended, axis=1)
    width_sum = head_sum(squares)
    width_mean = width_sum / (lax.axis_size("head") * head_depth)
    attention_part = attended * lax.rsqrt(width_mean + epsilon)[:, None] * attention_gain

    return call(
        renew_kernel,
        queries.shape,
        3 * 2**30,
        core_vector,
        own_sum,
        partner_sum,
        fast_gate,
        fast_up,
        fast_down,
        queries,
        attention_part,
        memory_gain,
    )


def solution(mesh):
    finer = Mesh(
        mesh.devices.reshape(4, 4, 4, 2, mesh.shape["head"]), ("y", "zh", "zl", "c", "head")
    )
    return jax.shard_map(
        on_device,
        mesh=finer,
        in_specs=(
            P("head", TOK, None),
            P("head", TOK, None),
            P("head", TOK, None),
            P("head", TOK),
            P("head", None, None),
            P("head", None, None),
            P("head", None, None),
            P("head", None),
            P("head", None),
        ),
        out_specs=P("head", TOK, None),
        check_vma=False,
    )
```

time: 102 us -> 83.1 us (0.81)
  starting transfers between devices: 27.8 us -> 46.2 us
  blocking collectives: 16.4 us -> 0 us
  waiting for transfers between devices: 34 us -> 23.6 us
  matrix products: 11.4 us -> 1.47 us
  Pallas kernels: 0 us -> 6.7 us
  local copies, waits for them, and re-layouts: 6.51 us -> 2.89 us
  between operations: 2.55 us -> 0.28 us
    ppermute x1 -> x5, starting transfers between devices: 3.7 us -> 27.6 us  [the longest x2 16 us: from_partner(): return lax.ppermute(array, PAIR, [(0, 1), (1, 0)])]
    all_gather x2 -> x0, blocking collectives: 16.4 us -> none  [the longest x1 8.97 us: on_device(): lax.all_gather(jnp.stack([keys, scaled, values]), PAIR, axis=1, tiled=True)]
    dot_general x30 -> x6, matrix products: 11.4 us -> 1.47 us  [dot(): lax.dot_general(a, b, (dims, ((), ())), preferred_element_type=jnp.float32)]
    all_to_all x4 -> x3, waiting for transfers between devices: 28.5 us -> 20.5 us  [exchange(): return lax.all_to_all(tiles, axis, split_axis=0, concat_axis=0, tiled=True)]
    pallas_call x0 -> x2, Pallas kernels: none -> 6.7 us  [call(): pl.pallas_call(kernel, out_shape=jax.ShapeDtypeStruct(shape, jnp.bfloat16...]
    all_to_all x4 -> x3, starting transfers between devices: 24.1 us -> 18.6 us  [exchange(): return lax.all_to_all(tiles, axis, split_axis=0, concat_axis=0, tiled=True)]
    ppermute x1 -> x5, waiting for transfers between devices: 5.51 us -> 3.03 us  [the longest x2 1.83 us: from_partner(): return lax.ppermute(array, PAIR, [(0, 1), (1, 0)])]
    unnamed x19 -> x18, local copies, waits for them, and re-layouts: 2.79 us -> 1.45 us
  transfers between devices with their start and end apart: 5 -> 8, of which waited for: 5 -> 5; matrix products, arithmetic and copies ran while one was open for 1% -> 3% of each run, Pallas kernels for 0% -> 0%
where the time goes in v2:
time: 83.1 us; the launch traced here: 82.5 us
  starting transfers between devices  46.2 us (56%)
  waiting for transfers between devices  23.6 us (28%)
  Pallas kernels  6.7 us (8%)
  local copies, waits for them, and re-layouts  2.89 us (3%)
  other arithmetic  1.48 us (2%)
  matrix products  1.47 us (2%)
    all_to_all x3, waiting for transfers between devices, exchange(): return lax.all_to_all(tiles, axis, split_axis=0, concat_axis=0, tiled=True)  20.5 us
    all_to_all x3, starting transfers between devices, exchange(): return lax.all_to_all(tiles, axis, split_axis=0, concat_axis=0, tiled=True)  18.6 us
    ppermute x2, starting transfers between devices, from_partner(): return lax.ppermute(array, PAIR, [(0, 1), (1, 0)])  16 us
    ppermute x2, starting transfers between devices, head_sum(): partial = partial + lax.ppermute(partial, 'head', pairs)  7.75 us
    pallas_call x2, Pallas kernels, call(): pl.pallas_call(kernel, out_shape=jax.ShapeDtypeStruct(shape, jnp.bfloat16...  6.7 us
    ppermute x1, starting transfers between devices, outer_halo(): return lax.ppermute(jnp.where(core == 0, first, last), TOK, swap)  3.82 us
    ppermute x2, waiting for transfers between devices, from_partner(): return lax.ppermute(array, PAIR, [(0, 1), (1, 0)])  1.83 us
  transfers between devices with their start and end apart: 8, of which 5 were waited for; matrix products, arithmetic and copies ran while one was open for 3% of the time, Pallas kernels for 0%

profile of v2, /device:TPU:1, one launch (start us, length us, event | category | flops | bytes accessed | tf_op | source)
XLA Modules:
  0.0 82.5 jit_solution(2680895345467911130)
XLA Ops:
  0.0 0.7 copy-done.7
  0.7 1.1 %multiply_convert_fusion = bf16[1,256,256]{2,1,0:T(8,128)(2,1)S(1)} fusion(bf16[1,256,256]{2,1,0:T(8,128)(2,1)} %param.11, f32[256]{0:T(256)S(1)} %bitcast.46), kind=kLoop, calls=%fused_computation.11 | loop fusion | flops 196608 | bytes 263168 | tf_op jit(solution)/shard_map/convert_element_type | solution.py:192
  1.8 0.0 copy-start.2
  1.9 8.9 %collective-permute-start = (bf16[3,256,256]{2,1,0:T(8,128)(2,1)S(1)}, bf16[3,256,256]{2,1,0:T(8,128)(2,1)S(1)}, u32[]{:S(2)}, u32[]{:S(2)}) collective-permute-start(bf16[3,256,256]{2,1,0:T(8,128)(2,1)S(1)} %pad_maximum_fusion.own_ref), channel_id=1, source_target_pairs={{0,4},{4,0},{1,5},{5,1},{2,6},{6,2},{3,7},{7,3},{8,12},{12,8},{9,1... | collective-permute-start | bytes 1179656 | tf_op jit(solution)/shard_map/ppermute | solution.py:45
  10.8 1.3 %collective-permute-done.partner_ref = bf16[3,256,256]{2,1,0:T(8,128)(2,1)S(1)} collective-permute-done((bf16[3,256,256]{2,1,0:T(8,128)(2,1)S(1)}, bf16[3,256,256]{2,1,0:T(8,128)(2,1)S(1)}, u32[]{:S(2)}, u32[]{:S(2)}) %collective-permute-start) | collective-permute-done | bytes 393248 | tf_op jit(solution)/shard_map/ppermute | solution.py:45
  12.1 1.7 %shard_map.94 = bf16[256,768]{1,0:T(8,128)(2,1)} custom-call(s32[1]{0:T(128)} %bitcast.core_ref, bf16[3,256,256]{2,1,0:T(8,128)(2,1)S(1)} %pad_maximum_fusion.own_ref, bf16[3,256,256]{2,1,0:T(8,128)(2,1)S(1)} %collective-permute-done.partner_ref, bf16[1,512,256]{2,1,0:T(8,128)(2,1)S(1)} %copy-done.1, bf16[1,512,256]{2,1,0:T(8,128)(2,1)S(1)} %copy-done.2, ...), custom_call_target="tpu_custom_call" | custom-call | flops 1073741824 | bytes 1048576 | tf_op jit(solution)/shard_map/pallas_call | solution.py:161
  13.8 3.6 %all-to-all-start = ((bf16[16,16,768]{2,1,0:T(8,128)(2,1)}), bf16[16,16,768]{2,1,0:T(8,128)(2,1)S(1)}, u32[]{:S(2)}, u32[]{:S(2)}) async-start(bf16[16,16,768]{2,1,0:T(8,128)(2,1)} %bitcast.2), calls=%async_computation | async-start | bytes 786432 | tf_op jit(solution)/shard_map/all_to_all | solution.py:49
  17.4 3.8 %collective-permute-start.2 = (bf16[2,128,256]{2,1,0:T(8,128)(2,1)S(1)}, bf16[2,128,256]{2,1,0:T(8,128)(2,1)S(1)}, u32[]{:S(2)}, u32[]{:S(2)}) collective-permute-start(bf16[2,128,256]{2,1,0:T(8,128)(2,1)S(1)} %maximum_select_fusion), channel_id=1, source_target_pairs={{4,8},{12,16},{20,24},{28,32},{36,40},{44,48},{52,56},{60,64},{68,... | collective-permute-start | bytes 393224 | tf_op jit(solution)/shard_map/ppermute | solution.py:41
  21.3 0.3 fusion.25
  21.5 8.9 %all-to-all-done = bf16[16,16,768]{2,1,0:T(8,128)(2,1)S(1)} async-done(((bf16[16,16,768]{2,1,0:T(8,128)(2,1)}), bf16[16,16,768]{2,1,0:T(8,128)(2,1)S(1)}, u32[]{:S(2)}, u32[]{:S(2)}) %all-to-all-start) | async-done | bytes 393248 | tf_op jit(solution)/shard_map/all_to_all | solution.py:49
  30.4 0.1 reduce_sum.60
  30.5 0.6 broadcast_in_dim.8
  31.1 11.4 %all-to-all-start.1 = ((bf16[4,16,768]{2,1,0:T(8,128)(2,1)}), bf16[4,16,768]{2,1,0:T(8,128)(2,1)S(1)}, u32[]{:S(2)}, u32[]{:S(2)}) async-start(bf16[4,16,768]{2,1,0:T(8,128)(2,1)} %broadcast_in_dim.8), calls=%async_computation.1 | async-start | bytes 196608 | tf_op jit(solution)/shard_map/all_to_all | solution.py:49
  42.6 0.2 fusion.24
  42.8 11.7 %all-to-all-done.1 = bf16[4,16,768]{2,1,0:T(8,128)(2,1)S(1)} async-done(((bf16[4,16,768]{2,1,0:T(8,128)(2,1)}), bf16[4,16,768]{2,1,0:T(8,128)(2,1)S(1)}, u32[]{:S(2)}, u32[]{:S(2)}) %all-to-all-start.1) | async-done | bytes 98336 | tf_op jit(solution)/shard_map/all_to_all | solution.py:49
  54.5 0.8 broadcast_in_dim.9
  55.3 3.6 %all-to-all-start.2 = ((bf16[16,16,768]{2,1,0:T(8,128)(2,1)}), bf16[16,16,768]{2,1,0:T(8,128)(2,1)S(1)}, u32[]{:S(2)}, u32[]{:S(2)}) async-start(bf16[16,16,768]{2,1,0:T(8,128)(2,1)} %broadcast_in_dim.9), calls=%async_computation.2 | async-start | bytes 786432 | tf_op jit(solution)/shard_map/all_to_all | solution.py:49
  58.8 0.2 fusion.26
  59.1 0.1 fusion.1
  59.1 0.1 fusion.9
  59.2 0.2 fusion.2
  59.5 0.2 convolution_add_fusion.1
  59.7 0.3 multiply_reduce_fusion
  60.0 3.1 %collective-permute-start.3 = (f32[256]{0:T(256)S(1)}, f32[256]{0:T(256)S(1)}, u32[]{:S(2)}, u32[]{:S(2)}) collective-permute-start(f32[256]{0:T(256)S(1)} %get-tuple-element.19), channel_id=1, source_target_pairs={{0,1},{1,0},{2,3},{3,2},{4,5},{5,4},{6,7},{7,6},{8,9},{9,8},{10,11... | collective-permute-start | bytes 3080 | tf_op jit(solution)/shard_map/ppermute | solution.py:62
  63.1 1.2 %collective-permute-done.3 = f32[256]{0:T(256)S(1)} collective-permute-done((f32[256]{0:T(256)S(1)}, f32[256]{0:T(256)S(1)}, u32[]{:S(2)}, u32[]{:S(2)}) %collective-permute-start.3) | collective-permute-done | bytes 1056 | tf_op jit(solution)/shard_map/ppermute | solution.py:62
  64.3 4.6 %collective-permute-start.4 = (f32[256]{0:T(256)S(1)}, f32[256]{0:T(256)S(1)}, u32[]{:S(2)}, u32[]{:S(2)}) collective-permute-start(f32[256]{0:T(256)S(1)} %add.55), channel_id=1, source_target_pairs={{0,2},{1,3},{2,0},{3,1},{4,6},{5,7},{6,4},{7,5},{8,10},{9,11},{10,... | collective-permute-start | bytes 3080 | tf_op jit(solution)/shard_map/ppermute | solution.py:62
  69.0 7.1 %collective-permute-start.1 = (bf16[256,768]{1,0:T(8,128)(2,1)S(1)}, bf16[256,768]{1,0:T(8,128)(2,1)S(1)}, u32[]{:S(2)}, u32[]{:S(2)}) collective-permute-start(bf16[256,768]{1,0:T(8,128)(2,1)S(1)} %bitcast.44), channel_id=1, source_target_pairs={{0,4},{4,0},{1,5},{5,1},{2,6},{6,2},{3,7},{7,3},{8,12},{12,8},{9,1... | collective-permute-start | bytes 1179656 | tf_op jit(solution)/shard_map/ppermute | solution.py:45
  76.2 0.7 copy-done.8
  76.8 0.1 multiply_multiply_fusion.attention_ref
  76.9 0.5 collective-permute-done.1.partner_ref
  77.5 0.1 copy-done.4
  77.5 5.0 %shard_map.95 = bf16[1,256,256]{2,1,0:T(8,128)(2,1)} custom-call(s32[1]{0:T(128)} %bitcast.core_ref, bf16[256,768]{1,0:T(8,128)(2,1)S(1)} %bitcast.45, bf16[256,768]{1,0:T(8,128)(2,1)S(1)} %collective-permute-done.1.partner_ref, bf16[1,512,256]{2,1,0:T(8,128)(2,1)S(1)} %copy-done.1, bf16[1,512,256]{2,1,0:T(8,128)(2,1)S(1)} %copy-done.2, ...), custom_call_target="tpu_custom_call" | custom-call | flops 3221225472 | bytes 1048576 | tf_op jit(solution)/shard_map/pallas_call | solution.py:161
  (26 shorter events, 0.2 us)
Async XLA Ops:
  0.0 0.7 copy-start.7
  0.7 1.1 %copy-start.5 = (bf16[1,256,256]{2,1,0:T(8,128)(2,1)S(1)}, bf16[1,256,256]{2,1,0:T(8,128)(2,1)}, u32[]{:S(2)}) copy-start(bf16[1,256,256]{2,1,0:T(8,128)(2,1)} %param.11) | copy-start | bytes 393220
  0.7 1.1 %copy-start.6 = (bf16[1,256,256]{2,1,0:T(8,128)(2,1)S(1)}, bf16[1,256,256]{2,1,0:T(8,128)(2,1)}, u32[]{:S(2)}) copy-start(bf16[1,256,256]{2,1,0:T(8,128)(2,1)} %param.10) | copy-start | bytes 393220
  1.8 10.3 %copy-start.1 = (bf16[1,512,256]{2,1,0:T(8,128)(2,1)S(1)}, bf16[1,512,256]{2,1,0:T(8,128)(2,1)}, u32[]{:S(2)}) copy-start(bf16[1,512,256]{2,1,0:T(8,128)(2,1)} %gate_ref.3) | copy-start | bytes 786436
  1.8 10.3 %copy-start.2 = (bf16[1,512,256]{2,1,0:T(8,128)(2,1)S(1)}, bf16[1,512,256]{2,1,0:T(8,128)(2,1)}, u32[]{:S(2)}) copy-start(bf16[1,512,256]{2,1,0:T(8,128)(2,1)} %up_ref.3) | copy-start | bytes 786436
  1.8 10.3 %copy-start.3 = (bf16[1,512,256]{2,1,0:T(8,128)(2,1)S(1)}, bf16[1,512,256]{2,1,0:T(8,128)(2,1)}, u32[]{:S(2)}) copy-start(bf16[1,512,256]{2,1,0:T(8,128)(2,1)} %down_ref.3) | copy-start | bytes 786436
  1.9 10.2 %collective-permute-start = (bf16[3,256,256]{2,1,0:T(8,128)(2,1)S(1)}, bf16[3,256,256]{2,1,0:T(8,128)(2,1)S(1)}, u32[]{:S(2)}, u32[]{:S(2)}) collective-permute-start(bf16[3,256,256]{2,1,0:T(8,128)(2,1)S(1)} %pad_maximum_fusion.own_ref), channel_id=1, source_target_pairs={{0,4},{4,0},{1,5},{5,1},{2,6},{6,2},{3,7},{7,3},{8,12},{12,8},{9,1... | collective-permute-start | bytes 1179656 | tf_op jit(solution)/shard_map/ppermute | solution.py:45
  13.8 16.6 %all-to-all-start = ((bf16[16,16,768]{2,1,0:T(8,128)(2,1)}), bf16[16,16,768]{2,1,0:T(8,128)(2,1)S(1)}, u32[]{:S(2)}, u32[]{:S(2)}) async-start(bf16[16,16,768]{2,1,0:T(8,128)(2,1)} %bitcast.2), calls=%async_computation | async-start | bytes 786432 | tf_op jit(solution)/shard_map/all_to_all | solution.py:49
  17.4 3.9 %copy-start = (bf16[1,256,256]{2,1,0:T(8,128)(2,1)S(1)}, bf16[1,256,256]{2,1,0:T(8,128)(2,1)}, u32[]{:S(2)}) copy-start(bf16[1,256,256]{2,1,0:T(8,128)(2,1)} %queries_ref.1) | copy-start | bytes 393220
  17.4 25.2 %collective-permute-start.2 = (bf16[2,128,256]{2,1,0:T(8,128)(2,1)S(1)}, bf16[2,128,256]{2,1,0:T(8,128)(2,1)S(1)}, u32[]{:S(2)}, u32[]{:S(2)}) collective-permute-start(bf16[2,128,256]{2,1,0:T(8,128)(2,1)S(1)} %maximum_select_fusion), channel_id=1, source_target_pairs={{4,8},{12,16},{20,24},{28,32},{36,40},{44,48},{52,56},{60,64},{68,... | collective-permute-start | bytes 393224 | tf_op jit(solution)/shard_map/ppermute | solution.py:41
  31.1 23.4 %all-to-all-start.1 = ((bf16[4,16,768]{2,1,0:T(8,128)(2,1)}), bf16[4,16,768]{2,1,0:T(8,128)(2,1)S(1)}, u32[]{:S(2)}, u32[]{:S(2)}) async-start(bf16[4,16,768]{2,1,0:T(8,128)(2,1)} %broadcast_in_dim.8), calls=%async_computation.1 | async-start | bytes 196608 | tf_op jit(solution)/shard_map/all_to_all | solution.py:49
  55.3 13.7 %all-to-all-start.2 = ((bf16[16,16,768]{2,1,0:T(8,128)(2,1)}), bf16[16,16,768]{2,1,0:T(8,128)(2,1)S(1)}, u32[]{:S(2)}, u32[]{:S(2)}) async-start(bf16[16,16,768]{2,1,0:T(8,128)(2,1)} %broadcast_in_dim.9), calls=%async_computation.2 | async-start | bytes 786432 | tf_op jit(solution)/shard_map/all_to_all | solution.py:49
  60.0 4.3 %collective-permute-start.3 = (f32[256]{0:T(256)S(1)}, f32[256]{0:T(256)S(1)}, u32[]{:S(2)}, u32[]{:S(2)}) collective-permute-start(f32[256]{0:T(256)S(1)} %get-tuple-element.19), channel_id=1, source_target_pairs={{0,1},{1,0},{2,3},{3,2},{4,5},{5,4},{6,7},{7,6},{8,9},{9,8},{10,11... | collective-permute-start | bytes 3080 | tf_op jit(solution)/shard_map/ppermute | solution.py:62
  64.3 11.8 %collective-permute-start.4 = (f32[256]{0:T(256)S(1)}, f32[256]{0:T(256)S(1)}, u32[]{:S(2)}, u32[]{:S(2)}) collective-permute-start(f32[256]{0:T(256)S(1)} %add.55), channel_id=1, source_target_pairs={{0,2},{1,3},{2,0},{3,1},{4,6},{5,7},{6,4},{7,5},{8,10},{9,11},{10,... | collective-permute-start | bytes 3080 | tf_op jit(solution)/shard_map/ppermute | solution.py:62
  69.0 8.5 %collective-permute-start.1 = (bf16[256,768]{1,0:T(8,128)(2,1)S(1)}, bf16[256,768]{1,0:T(8,128)(2,1)S(1)}, u32[]{:S(2)}, u32[]{:S(2)}) collective-permute-start(bf16[256,768]{1,0:T(8,128)(2,1)S(1)} %bitcast.44), channel_id=1, source_target_pairs={{0,4},{4,0},{1,5},{5,1},{2,6},{6,2},{3,7},{7,3},{8,12},{12,8},{9,1... | collective-permute-start | bytes 1179656 | tf_op jit(solution)/shard_map/ppermute | solution.py:45
  76.2 0.7 copy-start.8
  76.8 0.7 copy-start.4

commit v3 on v2

v3 whole, which is shorter than its diff:
```python
import functools

import jax
import jax.numpy as jnp
from jax import lax
from jax.experimental import pallas as pl
from jax.experimental.pallas import tpu as pltpu
from jax.sharding import Mesh
from jax.sharding import PartitionSpec as P


HALO = 128
NS_STEPS = 2
TOK = ("y", "zh", "zl", "c")
NEAR = ("y", "zl")
FAR = "zh"
PAIR = "c"
FAR_ORDER = [[2, 3, 0, 1]]

first_coeff = 3.4445
second_coeff = -4.775
third_coefficient = 2.0315
step_size = 1.0
norm_floor = 1e-07
epsilon = 1e-06
masked_score = -1e30

VMEM = pl.BlockSpec(memory_space=pltpu.VMEM)
SMEM = pl.BlockSpec(memory_space=pltpu.SMEM)
HBM = pl.BlockSpec(memory_space=pltpu.HBM)


def dot(a, b, dims):
    return lax.dot_general(a, b, (dims, ((), ())), preferred_element_type=jnp.float32)


def outer_halo(keys, values, core):
    count = lax.axis_size(TOK)
    ends = range(1, count - 1, 2)
    swap = [(i, i + 1) for i in ends] + [(i + 1, i) for i in ends]
    first = jnp.stack([keys[:HALO], values[:HALO]])
    last = jnp.stack([keys[-HALO:], values[-HALO:]])
    return lax.ppermute(jnp.where(core == 0, first, last), TOK, swap)


def from_partner(array):
    return lax.ppermute(array, PAIR, [(0, 1), (1, 0)])


def exchange(tiles, axis, groups=None):
    return lax.all_to_all(
        tiles, axis, split_axis=0, concat_axis=0, axis_index_groups=groups, tiled=True
    )


def copies_to(array, axis, groups=None):
    copies = jnp.broadcast_to(array, (lax.axis_size(axis), *array.shape))
    return exchange(copies, axis, groups)


def head_sum(partial):
    heads = lax.axis_size("head")
    distance = 1
    while distance < heads:
        pairs = [(i, i ^ distance) for i in range(heads)]
        partial = partial + lax.ppermute(partial, "head", pairs)
        distance *= 2
    return partial


def as_row(column):
    size = column.shape[0]
    diagonal = lax.broadcasted_iota(jnp.int32, (size, size), 0) == lax.broadcasted_iota(
        jnp.int32, (size, size), 1
    )
    return jnp.sum(jnp.where(diagonal, column, 0.0), axis=0, keepdims=True)


def as_column(row):
    size = row.shape[1]
    diagonal = lax.broadcasted_iota(jnp.int32, (size, size), 0) == lax.broadcasted_iota(
        jnp.int32, (size, size), 1
    )
    return jnp.sum(jnp.where(diagonal, row, 0.0), axis=1, keepdims=True)


def prepare_kernel(
    core_ref,
    keys_ref,
    values_ref,
    rate_ref,
    gate_ref,
    up_ref,
    down_ref,
    out_ref,
    weights_ref,
    rate,
    semaphores,
):
    half = weights_ref.shape[1]
    mine = pl.ds(pl.multiple_of(core_ref[0] * half, half), half)
    copies = [
        pltpu.make_async_copy(rate_ref, rate, semaphores.at[0]),
        pltpu.make_async_copy(values_ref.at[0], out_ref.at[2], semaphores.at[1]),
        pltpu.make_async_copy(keys_ref.at[0], out_ref.at[0], semaphores.at[2]),
    ]
    for i, ref in enumerate((gate_ref, up_ref, down_ref)):
        copies.append(
            pltpu.make_async_copy(ref.at[0, mine], weights_ref.at[i], semaphores.at[3 + i])
        )
    for copy in copies:
        copy.start()
    copies[0].wait()
    column = as_column(rate[...])
    copies[1].wait()
    out_ref[1] = (column * out_ref[2].astype(jnp.float32)).astype(jnp.bfloat16)
    for copy in copies[2:]:
        copy.wait()


def attention_kernel(
    core_ref, has_outer_ref, queries_ref, own_ref, partner_ref, outer_ref, out_ref, squares_ref
):
    near = pl.ds(pl.multiple_of(core_ref[0] * HALO, HALO), HALO)
    queries = queries_ref[0]
    scale = queries.shape[1] ** (-0.5)
    keys = (own_ref[0], partner_ref[0, near], outer_ref[0])
    values = (own_ref[2], partner_ref[2, near], outer_ref[1])
    scores = [dot(queries, k, ((1,), (1,))) * scale for k in keys]
    scores[2] = jnp.where(has_outer_ref[0] > 0, scores[2], masked_score)
    highest = functools.reduce(jnp.maximum, [jnp.max(s, axis=1, keepdims=True) for s in scores])
    weights = [jnp.exp(s - highest) for s in scores]
    total = sum(jnp.sum(w, axis=1, keepdims=True) for w in weights)
    attended = 0.0
    for w, v in zip(weights, values):
        attended += dot((w / total).astype(jnp.bfloat16), v, ((1,), (0,)))
    out_ref[...] = attended
    squares_ref[...] = as_row(jnp.sum(attended * attended, axis=1, keepdims=True))


def gradient_kernel(own_ref, partner_ref, weights_ref, out_ref):
    depth = weights_ref.shape[2]
    keys = jnp.concatenate([own_ref[0], partner_ref[0]], axis=0)
    scaled = jnp.concatenate([own_ref[1], partner_ref[1]], axis=0)
    gate_value = dot(keys, weights_ref[0], ((1,), (1,)))
    up_value = dot(keys, weights_ref[1], ((1,), (1,)))
    backward = dot(scaled, weights_ref[2], ((1,), (1,)))
    squashed = jax.nn.sigmoid(gate_value)
    silu = gate_value * squashed
    hidden = (silu * up_value).astype(jnp.bfloat16)
    gate_grad = (backward * up_value * squashed * (1.0 + gate_value * (1.0 - squashed))).astype(
        jnp.bfloat16
    )
    up_grad = (backward * silu).astype(jnp.bfloat16)
    pairs = ((gate_grad, keys), (up_grad, keys), (hidden, scaled))
    for i, (left, right) in enumerate(pairs):
        total = dot(left, right, ((0,), (0,)))
        out_ref[:, i * depth : (i + 1) * depth] = total.astype(jnp.bfloat16)


def renew_kernel(
    width,
    core_ref,
    own_ref,
    partner_ref,
    gate_ref,
    up_ref,
    down_ref,
    queries_ref,
    attended_ref,
    width_ref,
    attention_gain_ref,
    memory_gain_ref,
    out_ref,
    gains,
    semaphores,
):
    gain_copies = [
        pltpu.make_async_copy(ref, gains.at[i], semaphores.at[i])
        for i, ref in enumerate((attention_gain_ref, memory_gain_ref))
    ]
    for copy in gain_copies:
        copy.start()
    half = own_ref.shape[0]
    depth = gate_ref.shape[2]
    core = core_ref[0]
    rows = [pl.ds(pl.multiple_of(c * half, half), half) for c in (core, 1 - core)]
    diagonal = lax.broadcasted_iota(jnp.int32, (depth, depth), 0) == lax.broadcasted_iota(
        jnp.int32, (depth, depth), 1
    )
    current, rounded, grams = [], [], []
    for i in range(3):
        grads = jnp.concatenate(
            [ref[:, i * depth : (i + 1) * depth] for ref in (own_ref, partner_ref)], axis=0
        )
        gram = dot(grads, grads, ((0,), (0,)))
        trace = jnp.sum(jnp.where(diagonal, gram, 0.0), axis=0, keepdims=True)
        norm = jnp.sqrt(jnp.sum(trace, axis=1, keepdims=True))
        scaling = 1.0 / (norm + norm_floor)
        current.append(grads.astype(jnp.float32) * scaling)
        rounded.append(current[i].astype(jnp.bfloat16))
        grams.append(gram * scaling * scaling)
    for step in range(NS_STEPS):
        if step:
            grams = [dot(r, r, ((0,), (0,))) for r in rounded]
        mixers = []
        for gram in grams:
            low = gram.astype(jnp.bfloat16)
            squared = dot(low, low, ((1,), (0,)))
            mixers.append((second_coeff * gram + third_coefficient * squared).astype(jnp.bfloat16))
        current = [
            first_coeff * c + dot(r, m, ((1,), (0,))) for c, r, m in zip(current, rounded, mixers)
        ]
        rounded = [c.astype(jnp.bfloat16) for c in current]
    renewed = []
    for weights_ref, update in zip((gate_ref, up_ref, down_ref), current):
        weights = jnp.concatenate([weights_ref[0, r] for r in rows], axis=0).astype(jnp.float32)
        renewed.append((weights + step_size * update).astype(jnp.bfloat16))
    queries = queries_ref[0]
    gate_value = dot(queries, renewed[0], ((1,), (1,)))
    up_value = dot(queries, renewed[1], ((1,), (1,)))
    hidden = (gate_value * jax.nn.sigmoid(gate_value) * up_value).astype(jnp.bfloat16)
    memory = dot(hidden, renewed[2], ((1,), (0,)))
    mean = jnp.mean(memory * memory, axis=1, keepdims=True)
    width_scale = as_column(lax.rsqrt(width_ref[...] / width + epsilon))
    for copy in gain_copies:
        copy.wait()
    attention_part = attended_ref[...] * width_scale * gains[0]
    memory_part = memory * lax.rsqrt(mean + epsilon) * gains[1]
    out_ref[0] = (attention_part + memory_part).astype(jnp.bfloat16)


def in_hbm(*arrays):
    return [pltpu.with_memory_space_constraint(a, pltpu.HBM) for a in arrays]


def call(kernel, shapes, specs, flops, args, scratch=()):
    return pl.pallas_call(
        kernel,
        out_shape=shapes,
        in_specs=specs,
        out_specs=jax.tree.map(lambda _: VMEM, shapes),
        scratch_shapes=scratch,
        compiler_params=pltpu.CompilerParams(vmem_limit_bytes=32 * 2**20),
        cost_estimate=pl.CostEstimate(flops=flops, bytes_accessed=2**20, transcendentals=2**17),
    )(*args)


def on_device(
    queries,
    key_vectors,
    value_vectors,
    token_rate,
    fast_gate,
    fast_up,
    fast_down,
    attention_gain,
    memory_gain,
):
    rows, head_depth = key_vectors.shape[1:]
    hidden_units = fast_gate.shape[1]
    core = lax.axis_index(PAIR)
    core_vector = core.reshape(1)
    index = lax.axis_index(TOK)
    has_outer = jnp.where(core == 0, index > 0, index < lax.axis_size(TOK) - 1)
    narrow = functools.partial(jax.ShapeDtypeStruct, dtype=jnp.bfloat16)
    wide = functools.partial(jax.ShapeDtypeStruct, dtype=jnp.float32)

    half = hidden_units // 2
    own, weights = call(
        prepare_kernel,
        (narrow((3, rows, head_depth)), narrow((3, half, head_depth))),
        [SMEM] + [HBM] * 6,
        2**20,
        (
            core_vector,
            *in_hbm(key_vectors, value_vectors, token_rate, fast_gate, fast_up, fast_down),
        ),
        [pltpu.VMEM((1, rows), jnp.float32), pltpu.SemaphoreType.DMA((6,))],
    )
    partner = from_partner(own)
    grads = call(
        gradient_kernel, narrow((half, 3 * head_depth)), [VMEM] * 3, 2**30, (own, partner, weights)
    )
    near = lax.axis_size(NEAR)
    tiles = grads.reshape(near, half // near, 3 * head_depth)
    arrived = exchange(tiles, NEAR)
    sums = jnp.sum(arrived.astype(jnp.float32), axis=0).astype(jnp.bfloat16)
    arrived = copies_to(sums, FAR, FAR_ORDER)
    sums = jnp.sum(arrived.astype(jnp.float32), axis=0).astype(jnp.bfloat16)
    own_sum = copies_to(sums, NEAR).reshape(half, 3 * head_depth)
    partner_sum = from_partner(own_sum)

    outer = outer_halo(own[0], own[2], core)
    attended, squares = call(
        attention_kernel,
        (wide((rows, head_depth)), wide((1, rows))),
        [SMEM] * 2 + [VMEM] * 4,
        2**28,
        (core_vector, has_outer.astype(jnp.int32).reshape(1), queries, own, partner, outer),
    )
    width_sum = head_sum(squares)

    return call(
        functools.partial(renew_kernel, lax.axis_size("head") * head_depth),
        narrow(queries.shape),
        [SMEM] + [VMEM] * 8 + [HBM] * 2,
        3 * 2**30,
        (
            core_vector,
            own_sum,
            partner_sum,
            fast_gate,
            fast_up,
            fast_down,
            queries,
            attended,
            width_sum,
            *in_hbm(attention_gain, memory_gain),
        ),
        [pltpu.VMEM((2, 1, head_depth), jnp.float32), pltpu.SemaphoreType.DMA((2,))],
    )


def solution(mesh):
    finer = Mesh(
        mesh.devices.reshape(4, 4, 4, 2, mesh.shape["head"]), ("y", "zh", "zl", "c", "head")
    )
    return jax.shard_map(
        on_device,
        mesh=finer,
        in_specs=(
            P("head", TOK, None),
            P("head", TOK, None),
            P("head", TOK, None),
            P("head", TOK),
            P("head", None, None),
            P("head", None, None),
            P("head", None, None),
            P("head", None),
            P("head", None),
        ),
        out_specs=P("head", TOK, None),
        check_vma=False,
    )
```

time: 83.1 us -> 89 us (1.071)
  the two profiles are of different devices: /device:TPU:1 before, /device:TPU:28 now
where the time goes in v3:
time: 89 us; the launch traced here: 88.6 us
  blocking collectives  39.5 us (44%)
  starting transfers between devices  21.7 us (24%)
  waiting for transfers between devices  19.9 us (22%)
  Pallas kernels  6.39 us (7%)
    all_to_all x2, blocking collectives, exchange(): lax.all_to_all(tiles, axis, split_axis=0, concat_axis=0, axis_index_group...  39.5 us
    all_to_all x1, waiting for transfers between devices, exchange(): lax.all_to_all(tiles, axis, split_axis=0, concat_axis=0, axis_index_group...  8.72 us
    ppermute x2, waiting for transfers between devices, head_sum(): partial = partial + lax.ppermute(partial, 'head', pairs)  6.91 us
    ppermute x1, starting transfers between devices, outer_halo(): return lax.ppermute(jnp.where(core == 0, first, last), TOK, swap)  6.63 us
    pallas_call x4, Pallas kernels, call(): pl.pallas_call(kernel, out_shape=shapes, in_specs=specs, out_specs=jax.tr...  6.39 us
    all_to_all x1, starting transfers between devices, exchange(): lax.all_to_all(tiles, axis, split_axis=0, concat_axis=0, axis_index_group...  5.74 us
    ppermute x2, starting transfers between devices, head_sum(): partial = partial + lax.ppermute(partial, 'head', pairs)  5.5 us
    ppermute x2, starting transfers between devices, from_partner(): return lax.ppermute(array, PAIR, [(0, 1), (1, 0)])  3.83 us
  transfers between devices with their start and end apart: 6, of which 5 were waited for; matrix products, arithmetic and copies ran while one was open for 0% of the time, Pallas kernels for 1%

profile of v3, /device:TPU:28, one launch (start us, length us, event | category | flops | bytes accessed | tf_op | source)
XLA Modules:
  0.0 88.6 jit_solution(9557363532266255416)
XLA Ops:
  0.0 1.2 %shard_map.91 = (bf16[3,256,256]{2,1,0:T(8,128)(2,1)S(1)}, bf16[3,256,256]{2,1,0:T(8,128)(2,1)S(1)}) custom-call(s32[1]{0:T(128)} %bitcast.core_ref, bf16[1,256,256]{2,1,0:T(8,128)(2,1)} %keys_ref.1, bf16[1,256,256]{2,1,0:T(8,128)(2,1)} %values_ref.1, f32[1,256]{1,0:T(1,128)} %rate_ref.1, bf16[1,512,256]{2,1,0:T(8,128)(2,1)} %gate_ref.3, ...), custom_call_target="tpu_custom_call" | custom-call | flops 1048576 | bytes 1048576 | tf_op jit(solution)/shard_map/pallas_call | solution.py:238
  1.2 1.9 %collective-permute-start = (bf16[3,256,256]{2,1,0:T(8,128)(2,1)S(1)}, bf16[3,256,256]{2,1,0:T(8,128)(2,1)S(1)}, u32[]{:S(2)}, u32[]{:S(2)}) collective-permute-start(bf16[3,256,256]{2,1,0:T(8,128)(2,1)S(1)} %get-tuple-element.9.own_ref), channel_id=1, source_target_pairs={{0,4},{4,0},{1,5},{5,1},{2,6},{6,2},{3,7},{7,3},{8,12},{12,8},{9,1... | collective-permute-start | bytes 1179656 | tf_op jit(solution)/shard_map/ppermute | solution.py:47
  3.2 1.7 %collective-permute-done.partner_ref = bf16[3,256,256]{2,1,0:T(8,128)(2,1)S(1)} collective-permute-done((bf16[3,256,256]{2,1,0:T(8,128)(2,1)S(1)}, bf16[3,256,256]{2,1,0:T(8,128)(2,1)S(1)}, u32[]{:S(2)}, u32[]{:S(2)}) %collective-permute-start) | collective-permute-done | bytes 393248 | tf_op jit(solution)/shard_map/ppermute | solution.py:47
  4.9 0.9 %shard_map.92 = bf16[256,768]{1,0:T(8,128)(2,1)S(1)} custom-call(bf16[3,256,256]{2,1,0:T(8,128)(2,1)S(1)} %get-tuple-element.9.own_ref, bf16[3,256,256]{2,1,0:T(8,128)(2,1)S(1)} %collective-permute-done.partner_ref, bf16[3,256,256]{2,1,0:T(8,128)(2,1)S(1)} %get-tuple-element.10.weights_ref), custom_call_target="tpu_custom_call" | custom-call | flops 1073741824 | bytes 1048576 | tf_op jit(solution)/shard_map/pallas_call | solution.py:238
  5.7 20.3 %all_to_all.15 = bf16[16,16,768]{2,1,0:T(8,128)(2,1)S(1)} all-to-all(bf16[16,16,768]{2,1,0:T(8,128)(2,1)S(1)} %bitcast.6), channel_id=1, replica_groups=mesh['y'=4,'zh'=4,'zl'=4,'c'=2,'head'=4] {'y','zl'}, dimensions={0} | all-to-all | bytes 786432 | tf_op jit(solution)/shard_map/all_to_all | solution.py:51
  26.0 0.1 reduce_sum.24
  26.1 19.2 %all_to_all.16 = bf16[4,16,768]{2,1,0:T(8,128)(2,1)S(1)} all-to-all(bf16[4,16,768]{2,1,0:T(8,128)(2,1)S(1)} %broadcast_in_dim.6), channel_id=1, replica_groups={{64,96,0,32},{65,97,1,33},{66,98,2,34},{67,99,3,35},{68,100,4,36},{69,1..., dimensions={0} | all-to-all | bytes 196608 | tf_op jit(solution)/shard_map/all_to_all | solution.py:51
  45.3 0.8 broadcast_in_dim.7
  46.1 5.7 %all-to-all-start.2 = ((bf16[16,16,768]{2,1,0:T(8,128)(2,1)}), bf16[16,16,768]{2,1,0:T(8,128)(2,1)S(1)}, u32[]{:S(2)}, u32[]{:S(2)}) async-start(bf16[16,16,768]{2,1,0:T(8,128)(2,1)} %broadcast_in_dim.7), calls=%async_computation.2 | async-start | bytes 786432 | tf_op jit(solution)/shard_map/all_to_all | solution.py:51
  51.9 8.7 %all-to-all-done.2 = bf16[16,16,768]{2,1,0:T(8,128)(2,1)S(1)} async-done(((bf16[16,16,768]{2,1,0:T(8,128)(2,1)}), bf16[16,16,768]{2,1,0:T(8,128)(2,1)S(1)}, u32[]{:S(2)}, u32[]{:S(2)}) %all-to-all-start.2) | async-done | bytes 393248 | tf_op jit(solution)/shard_map/all_to_all | solution.py:51
  60.6 1.9 %collective-permute-start.1 = (bf16[256,768]{1,0:T(8,128)(2,1)S(1)}, bf16[256,768]{1,0:T(8,128)(2,1)S(1)}, u32[]{:S(2)}, u32[]{:S(2)}) collective-permute-start(bf16[256,768]{1,0:T(8,128)(2,1)S(1)} %bitcast.4), channel_id=1, source_target_pairs={{0,4},{4,0},{1,5},{5,1},{2,6},{6,2},{3,7},{7,3},{8,12},{12,8},{9,1... | collective-permute-start | bytes 1179656 | tf_op jit(solution)/shard_map/ppermute | solution.py:47
  62.5 0.0 copy-start.3
  62.6 6.6 %collective-permute-start.2 = (bf16[2,128,256]{2,1,0:T(8,128)(2,1)S(1)}, bf16[2,128,256]{2,1,0:T(8,128)(2,1)S(1)}, u32[]{:S(2)}, u32[]{:S(2)}) collective-permute-start(bf16[2,128,256]{2,1,0:T(8,128)(2,1)S(1)} %maximum_select_fusion), channel_id=1, source_target_pairs={{4,8},{12,16},{20,24},{28,32},{36,40},{44,48},{52,56},{60,64},{68,... | collective-permute-start | bytes 393224 | tf_op jit(solution)/shard_map/ppermute | solution.py:43
  69.2 2.6 %collective-permute-done.2.outer_ref = bf16[2,128,256]{2,1,0:T(8,128)(2,1)S(1)} collective-permute-done((bf16[2,128,256]{2,1,0:T(8,128)(2,1)S(1)}, bf16[2,128,256]{2,1,0:T(8,128)(2,1)S(1)}, u32[]{:S(2)}, u32[]{:S(2)}) %collective-permute-start.2) | collective-permute-done | bytes 131104 | tf_op jit(solution)/shard_map/ppermute | solution.py:43
  71.8 0.0 copy-done.3
  71.8 0.0 copy-start
  71.8 0.0 copy-start.1
  71.8 0.0 copy-start.2
  71.9 0.9 %shard_map.93 = (f32[256,256]{1,0:T(8,128)S(1)}, f32[1,256]{1,0:T(1,128)S(1)}) custom-call(s32[1]{0:T(128)} %bitcast.core_ref, s32[1]{0:T(128)} %bitcast.3.has_outer_ref, bf16[1,256,256]{2,1,0:T(8,128)(2,1)S(1)} %copy-done.3, bf16[3,256,256]{2,1,0:T(8,128)(2,1)S(1)} %get-tuple-element.9.own_ref, bf16[3,256,256]{2,1,0:T(8,128)(2,1)S(1)} %collective-permute-done.partner_ref, ...), custom_call_target="tpu_custom_call" | custom-call | flops 268435456 | bytes 1048576 | tf_op jit(solution)/shard_map/pallas_call | solution.py:238
  72.8 3.1 %collective-permute-start.3 = (f32[1,256]{1,0:T(1,128)S(1)}, f32[1,256]{1,0:T(1,128)S(1)}, u32[]{:S(2)}, u32[]{:S(2)}) collective-permute-start(f32[1,256]{1,0:T(1,128)S(1)} %get-tuple-element.12), channel_id=1, source_target_pairs={{0,1},{1,0},{2,3},{3,2},{4,5},{5,4},{6,7},{7,6},{8,9},{9,8},{10,11... | collective-permute-start | bytes 3080 | tf_op jit(solution)/shard_map/ppermute | solution.py:66
  75.9 2.4 %collective-permute-done.3 = f32[1,256]{1,0:T(1,128)S(1)} collective-permute-done((f32[1,256]{1,0:T(1,128)S(1)}, f32[1,256]{1,0:T(1,128)S(1)}, u32[]{:S(2)}, u32[]{:S(2)}) %collective-permute-start.3) | collective-permute-done | bytes 1056 | tf_op jit(solution)/shard_map/ppermute | solution.py:66
  78.2 2.4 %collective-permute-start.4 = (f32[1,256]{1,0:T(1,128)S(1)}, f32[1,256]{1,0:T(1,128)S(1)}, u32[]{:S(2)}, u32[]{:S(2)}) collective-permute-start(f32[1,256]{1,0:T(1,128)S(1)} %add.18), channel_id=1, source_target_pairs={{0,2},{1,3},{2,0},{3,1},{4,6},{5,7},{6,4},{7,5},{8,10},{9,11},{10,... | collective-permute-start | bytes 3080 | tf_op jit(solution)/shard_map/ppermute | solution.py:66
  80.7 4.6 %collective-permute-done.4 = f32[1,256]{1,0:T(1,128)S(1)} collective-permute-done((f32[1,256]{1,0:T(1,128)S(1)}, f32[1,256]{1,0:T(1,128)S(1)}, u32[]{:S(2)}, u32[]{:S(2)}) %collective-permute-start.4) | collective-permute-done | bytes 1056 | tf_op jit(solution)/shard_map/ppermute | solution.py:66
  85.2 0.0 collective-permute-done.1.partner_ref
  85.2 0.0 copy-done
  85.2 0.0 copy-done.1
  85.2 0.0 copy-done.2
  85.2 3.4 %shard_map.94 = bf16[1,256,256]{2,1,0:T(8,128)(2,1)} custom-call(s32[1]{0:T(128)} %bitcast.core_ref, bf16[256,768]{1,0:T(8,128)(2,1)S(1)} %bitcast.5, bf16[256,768]{1,0:T(8,128)(2,1)S(1)} %collective-permute-done.1.partner_ref, bf16[1,512,256]{2,1,0:T(8,128)(2,1)S(1)} %copy-done, bf16[1,512,256]{2,1,0:T(8,128)(2,1)S(1)} %copy-done.1, ...), custom_call_target="tpu_custom_call" | custom-call | flops 3221225472 | bytes 1048576 | tf_op jit(solution)/shard_map/pallas_call | solution.py:238
  (6 shorter events, 0.1 us)
Async XLA Ops:
  1.2 3.6 %collective-permute-start = (bf16[3,256,256]{2,1,0:T(8,128)(2,1)S(1)}, bf16[3,256,256]{2,1,0:T(8,128)(2,1)S(1)}, u32[]{:S(2)}, u32[]{:S(2)}) collective-permute-start(bf16[3,256,256]{2,1,0:T(8,128)(2,1)S(1)} %get-tuple-element.9.own_ref), channel_id=1, source_target_pairs={{0,4},{4,0},{1,5},{5,1},{2,6},{6,2},{3,7},{7,3},{8,12},{12,8},{9,1... | collective-permute-start | bytes 1179656 | tf_op jit(solution)/shard_map/ppermute | solution.py:47
  46.1 14.5 %all-to-all-start.2 = ((bf16[16,16,768]{2,1,0:T(8,128)(2,1)}), bf16[16,16,768]{2,1,0:T(8,128)(2,1)S(1)}, u32[]{:S(2)}, u32[]{:S(2)}) async-start(bf16[16,16,768]{2,1,0:T(8,128)(2,1)} %broadcast_in_dim.7), calls=%async_computation.2 | async-start | bytes 786432 | tf_op jit(solution)/shard_map/all_to_all | solution.py:51
  60.6 24.6 %collective-permute-start.1 = (bf16[256,768]{1,0:T(8,128)(2,1)S(1)}, bf16[256,768]{1,0:T(8,128)(2,1)S(1)}, u32[]{:S(2)}, u32[]{:S(2)}) collective-permute-start(bf16[256,768]{1,0:T(8,128)(2,1)S(1)} %bitcast.4), channel_id=1, source_target_pairs={{0,4},{4,0},{1,5},{5,1},{2,6},{6,2},{3,7},{7,3},{8,12},{12,8},{9,1... | collective-permute-start | bytes 1179656 | tf_op jit(solution)/shard_map/ppermute | solution.py:47
  62.5 9.3 %copy-start.3 = (bf16[1,256,256]{2,1,0:T(8,128)(2,1)S(1)}, bf16[1,256,256]{2,1,0:T(8,128)(2,1)}, u32[]{:S(2)}) copy-start(bf16[1,256,256]{2,1,0:T(8,128)(2,1)} %queries_ref.3) | copy-start | bytes 393220
  62.6 9.3 %collective-permute-start.2 = (bf16[2,128,256]{2,1,0:T(8,128)(2,1)S(1)}, bf16[2,128,256]{2,1,0:T(8,128)(2,1)S(1)}, u32[]{:S(2)}, u32[]{:S(2)}) collective-permute-start(bf16[2,128,256]{2,1,0:T(8,128)(2,1)S(1)} %maximum_select_fusion), channel_id=1, source_target_pairs={{4,8},{12,16},{20,24},{28,32},{36,40},{44,48},{52,56},{60,64},{68,... | collective-permute-start | bytes 393224 | tf_op jit(solution)/shard_map/ppermute | solution.py:43
  71.8 13.4 %copy-start = (bf16[1,512,256]{2,1,0:T(8,128)(2,1)S(1)}, bf16[1,512,256]{2,1,0:T(8,128)(2,1)}, u32[]{:S(2)}) copy-start(bf16[1,512,256]{2,1,0:T(8,128)(2,1)} %gate_ref.3) | copy-start | bytes 786436
  71.8 13.4 %copy-start.1 = (bf16[1,512,256]{2,1,0:T(8,128)(2,1)S(1)}, bf16[1,512,256]{2,1,0:T(8,128)(2,1)}, u32[]{:S(2)}) copy-start(bf16[1,512,256]{2,1,0:T(8,128)(2,1)} %up_ref.3) | copy-start | bytes 786436
  71.8 13.4 %copy-start.2 = (bf16[1,512,256]{2,1,0:T(8,128)(2,1)S(1)}, bf16[1,512,256]{2,1,0:T(8,128)(2,1)}, u32[]{:S(2)}) copy-start(bf16[1,512,256]{2,1,0:T(8,128)(2,1)} %down_ref.3) | copy-start | bytes 786436
  72.8 5.5 %collective-permute-start.3 = (f32[1,256]{1,0:T(1,128)S(1)}, f32[1,256]{1,0:T(1,128)S(1)}, u32[]{:S(2)}, u32[]{:S(2)}) collective-permute-start(f32[1,256]{1,0:T(1,128)S(1)} %get-tuple-element.12), channel_id=1, source_target_pairs={{0,1},{1,0},{2,3},{3,2},{4,5},{5,4},{6,7},{7,6},{8,9},{9,8},{10,11... | collective-permute-start | bytes 3080 | tf_op jit(solution)/shard_map/ppermute | solution.py:66
  78.2 7.0 %collective-permute-start.4 = (f32[1,256]{1,0:T(1,128)S(1)}, f32[1,256]{1,0:T(1,128)S(1)}, u32[]{:S(2)}, u32[]{:S(2)}) collective-permute-start(f32[1,256]{1,0:T(1,128)S(1)} %add.18), channel_id=1, source_target_pairs={{0,2},{1,3},{2,0},{3,1},{4,6},{5,7},{6,4},{7,5},{8,10},{9,11},{10,... | collective-permute-start | bytes 3080 | tf_op jit(solution)/shard_map/ppermute | solution.py:66

commit v4 on v3

--- a/solution.py
+++ b/solution.py
@@ -16,6 +16,7 @@
 FAR = "zh"
 PAIR = "c"
 FAR_ORDER = [[2, 3, 0, 1]]
+NEAR_ORDER = [[(i + 8) % 16 for i in range(16)]]
 
 first_coeff = 3.4445
 second_coeff = -4.775
@@ -60,11 +61,11 @@
 
 def head_sum(partial):
     heads = lax.axis_size("head")
-    distance = 1
-    while distance < heads:
-        pairs = [(i, i ^ distance) for i in range(heads)]
+    step = 1
+    while 2**step <= heads:
+        pairs = [(i, i ^ (2**step - 1)) for i in range(heads)]
         partial = partial + lax.ppermute(partial, "head", pairs)
-        distance *= 2
+        step += 1
     return partial
 
 
@@ -119,8 +120,25 @@
 
 
 def attention_kernel(
-    core_ref, has_outer_ref, queries_ref, own_ref, partner_ref, outer_ref, out_ref, squares_ref
+    core_ref,
+    has_outer_ref,
+    queries_ref,
+    own_ref,
+    partner_ref,
+    outer_ref,
+    attention_gain_ref,
+    memory_gain_ref,
+    out_ref,
+    squares_ref,
+    gains_ref,
+    semaphores,
 ):
+    gain_copies = [
+        pltpu.make_async_copy(ref, gains_ref.at[i], semaphores.at[i])
+        for i, ref in enumerate((attention_gain_ref, memory_gain_ref))
+    ]
+    for copy in gain_copies:
+        copy.start()
     near = pl.ds(pl.multiple_of(core_ref[0] * HALO, HALO), HALO)
     queries = queries_ref[0]
     scale = queries.shape[1] ** (-0.5)
@@ -136,64 +154,72 @@
         attended += dot((w / total).astype(jnp.bfloat16), v, ((1,), (0,)))
     out_ref[...] = attended
     squares_ref[...] = as_row(jnp.sum(attended * attended, axis=1, keepdims=True))
-
-
-def gradient_kernel(own_ref, partner_ref, weights_ref, out_ref):
-    depth = weights_ref.shape[2]
-    keys = jnp.concatenate([own_ref[0], partner_ref[0]], axis=0)
-    scaled = jnp.concatenate([own_ref[1], partner_ref[1]], axis=0)
+    for copy in gain_copies:
+        copy.wait()
+
+
+def signals(keys, scaled, weights_ref):
     gate_value = dot(keys, weights_ref[0], ((1,), (1,)))
     up_value = dot(keys, weights_ref[1], ((1,), (1,)))
     backward = dot(scaled, weights_ref[2], ((1,), (1,)))
     squashed = jax.nn.sigmoid(gate_value)
     silu = gate_value * squashed
-    hidden = (silu * up_value).astype(jnp.bfloat16)
-    gate_grad = (backward * up_value * squashed * (1.0 + gate_value * (1.0 - squashed))).astype(
-        jnp.bfloat16
-    )
-    up_grad = (backward * silu).astype(jnp.bfloat16)
-    pairs = ((gate_grad, keys), (up_grad, keys), (hidden, scaled))
-    for i, (left, right) in enumerate(pairs):
-        total = dot(left, right, ((0,), (0,)))
-        out_ref[:, i * depth : (i + 1) * depth] = total.astype(jnp.bfloat16)
+    gate_grad = backward * up_value * squashed * (1.0 + gate_value * (1.0 - squashed))
+    return [x.astype(jnp.bfloat16) for x in (gate_grad, backward * silu, silu * up_value)]
+
+
+def signal_kernel(own_ref, weights_ref, out_ref, turned_ref):
+    for i, x in enumerate(signals(own_ref[0], own_ref[1], weights_ref)):
+        out_ref[i] = x
+    for i in range(2):
+        turned_ref[i] = own_ref[i].T
+
+
+def gradient_kernel(partner_ref, weights_ref, signals_ref, turned_ref, out_ref):
+    half = weights_ref.shape[1]
+    turned = [
+        jnp.concatenate([turned_ref[i], partner_ref[i].T], axis=1) for i in range(2)
+    ]
+    for i, right in enumerate(signals(partner_ref[0], partner_ref[1], weights_ref)):
+        total = dot(
+            turned[1 if i == 2 else 0],
+            jnp.concatenate([signals_ref[i], right], axis=0),
+            ((1,), (0,)),
+        )
+        out_ref[:, i * half : (i + 1) * half] = total.astype(jnp.bfloat16)
+
+
+def turn_kernel(core_ref, gate_ref, up_ref, down_ref, out_ref):
+    half = gate_ref.shape[1] // 2
+    core = core_ref[0]
+    for i, ref in enumerate((gate_ref, up_ref, down_ref)):
+        for j, c in enumerate((core, 1 - core)):
+            rows = ref[0, pl.ds(pl.multiple_of(c * half, half), half)]
+            out_ref[i, :, j * half : (j + 1) * half] = rows.T
 
 
 def renew_kernel(
     width,
-    core_ref,
     own_ref,
     partner_ref,
-    gate_ref,
-    up_ref,
-    down_ref,
+    turned_ref,
     queries_ref,
     attended_ref,
     width_ref,
-    attention_gain_ref,
-    memory_gain_ref,
+    gains_ref,
     out_ref,
-    gains,
-    semaphores,
 ):
-    gain_copies = [
-        pltpu.make_async_copy(ref, gains.at[i], semaphores.at[i])
-        for i, ref in enumerate((attention_gain_ref, memory_gain_ref))
-    ]
-    for copy in gain_copies:
-        copy.start()
-    half = own_ref.shape[0]
-    depth = gate_ref.shape[2]
-    core = core_ref[0]
-    rows = [pl.ds(pl.multiple_of(c * half, half), half) for c in (core, 1 - core)]
+    depth = own_ref.shape[0]
+    half = turned_ref.shape[2] // 2
     diagonal = lax.broadcasted_iota(jnp.int32, (depth, depth), 0) == lax.broadcasted_iota(
         jnp.int32, (depth, depth), 1
     )
     current, rounded, grams = [], [], []
     for i in range(3):
         grads = jnp.concatenate(
-            [ref[:, i * depth : (i + 1) * depth] for ref in (own_ref, partner_ref)], axis=0
+            [ref[:, i * half : (i + 1) * half] for ref in (own_ref, partner_ref)], axis=1
         )
-        gram = dot(grads, grads, ((0,), (0,)))
+        gram = dot(grads, grads, ((1,), (1,)))
         trace = jnp.sum(jnp.where(diagonal, gram, 0.0), axis=0, keepdims=True)
         norm = jnp.sqrt(jnp.sum(trace, axis=1, keepdims=True))
         scaling = 1.0 / (norm + norm_floor)
@@ -202,31 +228,29 @@
         grams.append(gram * scaling * scaling)
     for step in range(NS_STEPS):
         if step:
-            grams = [dot(r, r, ((0,), (0,))) for r in rounded]
+            grams = [dot(r, r, ((1,), (1,))) for r in rounded]
         mixers = []
         for gram in grams:
             low = gram.astype(jnp.bfloat16)
             squared = dot(low, low, ((1,), (0,)))
             mixers.append((second_coeff * gram + third_coefficient * squared).astype(jnp.bfloat16))
         current = [
-            first_coeff * c + dot(r, m, ((1,), (0,))) for c, r, m in zip(current, rounded, mixers)
+            first_coeff * c + dot(m, r, ((1,), (0,))) for c, r, m in zip(current, rounded, mixers)
         ]
         rounded = [c.astype(jnp.bfloat16) for c in current]
-    renewed = []
-    for weights_ref, update in zip((gate_ref, up_ref, down_ref), current):
-        weights = jnp.concatenate([weights_ref[0, r] for r in rows], axis=0).astype(jnp.float32)
-        renewed.append((weights + step_size * update).astype(jnp.bfloat16))
+    renewed = [
+        (turned_ref[i].astype(jnp.float32) + step_size * c).astype(jnp.bfloat16)
+        for i, c in enumerate(current)
+    ]
     queries = queries_ref[0]
-    gate_value = dot(queries, renewed[0], ((1,), (1,)))
-    up_value = dot(queries, renewed[1], ((1,), (1,)))
+    gate_value = dot(queries, renewed[0], ((1,), (0,)))
+    up_value = dot(queries, renewed[1], ((1,), (0,)))
     hidden = (gate_value * jax.nn.sigmoid(gate_value) * up_value).astype(jnp.bfloat16)
-    memory = dot(hidden, renewed[2], ((1,), (0,)))
+    memory = dot(hidden, renewed[2], ((1,), (1,)))
     mean = jnp.mean(memory * memory, axis=1, keepdims=True)
     width_scale = as_column(lax.rsqrt(width_ref[...] / width + epsilon))
-    for copy in gain_copies:
-        copy.wait()
-    attention_part = attended_ref[...] * width_scale * gains[0]
-    memory_part = memory * lax.rsqrt(mean + epsilon) * gains[1]
+    attention_part = attended_ref[...] * width_scale * gains_ref[0]
+    memory_part = memory * lax.rsqrt(mean + epsilon) * gains_ref[1]
     out_ref[0] = (attention_part + memory_part).astype(jnp.bfloat16)
 
 
@@ -279,46 +303,61 @@
         [pltpu.VMEM((1, rows), jnp.float32), pltpu.SemaphoreType.DMA((6,))],
     )
     partner = from_partner(own)
+    own_signals, own_turned = call(
+        signal_kernel,
+        (narrow((3, rows, half)), narrow((2, head_depth, rows))),
+        [VMEM] * 2,
+        2**29,
+        (own, weights),
+    )
     grads = call(
-        gradient_kernel, narrow((half, 3 * head_depth)), [VMEM] * 3, 2**30, (own, partner, weights)
+        gradient_kernel,
+        narrow((head_depth, 3 * half)),
+        [VMEM] * 4,
+        2**30,
+        (partner, weights, own_signals, own_turned),
+    )
+    turned = call(
+        turn_kernel,
+        narrow((3, head_depth, hidden_units)),
+        [SMEM] + [VMEM] * 3,
+        2**27,
+        (core_vector, fast_gate, fast_up, fast_down),
     )
     near = lax.axis_size(NEAR)
-    tiles = grads.reshape(near, half // near, 3 * head_depth)
-    arrived = exchange(tiles, NEAR)
+    tiles = grads.reshape(near, head_depth // near, 3 * half)
+    arrived = exchange(tiles, NEAR, NEAR_ORDER)
     sums = jnp.sum(arrived.astype(jnp.float32), axis=0).astype(jnp.bfloat16)
     arrived = copies_to(sums, FAR, FAR_ORDER)
     sums = jnp.sum(arrived.astype(jnp.float32), axis=0).astype(jnp.bfloat16)
-    own_sum = copies_to(sums, NEAR).reshape(half, 3 * head_depth)
+    own_sum = copies_to(sums, NEAR, NEAR_ORDER).reshape(grads.shape)
     partner_sum = from_partner(own_sum)
 
     outer = outer_halo(own[0], own[2], core)
-    attended, squares = call(
+    attended, squares, gains = call(
         attention_kernel,
-        (wide((rows, head_depth)), wide((1, rows))),
-        [SMEM] * 2 + [VMEM] * 4,
+        (wide((rows, head_depth)), wide((1, rows)), wide((2, 1, head_depth))),
+        [SMEM] * 2 + [VMEM] * 4 + [HBM] * 2,
         2**28,
-        (core_vector, has_outer.astype(jnp.int32).reshape(1), queries, own, partner, outer),
+        (
+            core_vector,
+            has_outer.astype(jnp.int32).reshape(1),
+            queries,
+            own,
+            partner,
+            outer,
+            *in_hbm(attention_gain, memory_gain),
+        ),
+        [pltpu.SemaphoreType.DMA((2,))],
     )
     width_sum = head_sum(squares)
 
     return call(
         functools.partial(renew_kernel, lax.axis_size("head") * head_depth),
         narrow(queries.shape),
-        [SMEM] + [VMEM] * 8 + [HBM] * 2,
+        [VMEM] * 7,
         3 * 2**30,
-        (
-            core_vector,
-            own_sum,
-            partner_sum,
-            fast_gate,
-            fast_up,
-            fast_down,
-            queries,
-            attended,
-            width_sum,
-            *in_hbm(attention_gain, memory_gain),
-        ),
-        [pltpu.VMEM((2, 1, head_depth), jnp.float32), pltpu.SemaphoreType.DMA((2,))],
+        (own_sum, partner_sum, turned, queries, attended, width_sum, gains),
     )
 
 

time: 89 us -> 87.6 us (0.984)
  the two profiles are of different devices: /device:TPU:28 before, /device:TPU:14 now
where the time goes in v4:
time: 87.6 us; the launch traced here: 87.3 us
  blocking collectives  54.5 us (62%)
  starting transfers between devices  15.1 us (17%)
  waiting for transfers between devices  10.7 us (12%)
  Pallas kernels  6.63 us (8%)
    all_to_all x3, blocking collectives, exchange(): lax.all_to_all(tiles, axis, split_axis=0, concat_axis=0, axis_index_group...  54.5 us
    ppermute x2, waiting for transfers between devices, head_sum(): partial = partial + lax.ppermute(partial, 'head', pairs)  6.72 us
    pallas_call x6, Pallas kernels, call(): pl.pallas_call(kernel, out_shape=shapes, in_specs=specs, out_specs=jax.tr...  6.63 us
    ppermute x1, starting transfers between devices, outer_halo(): return lax.ppermute(jnp.where(core == 0, first, last), TOK, swap)  6.13 us
    ppermute x2, starting transfers between devices, head_sum(): partial = partial + lax.ppermute(partial, 'head', pairs)  5.11 us
    ppermute x2, starting transfers between devices, from_partner(): return lax.ppermute(array, PAIR, [(0, 1), (1, 0)])  3.83 us
    ppermute x1, waiting for transfers between devices, outer_halo(): return lax.ppermute(jnp.where(core == 0, first, last), TOK, swap)  2.61 us
  transfers between devices with their start and end apart: 5, of which 4 were waited for; matrix products, arithmetic and copies ran while one was open for 0% of the time, Pallas kernels for 2%

profile of v4, /device:TPU:14, one launch (start us, length us, event | category | flops | bytes accessed | tf_op | source)
XLA Modules:
  0.0 87.3 jit_solution(7022172928124027503)
XLA Ops:
  0.0 1.2 %shard_map.91 = (bf16[3,256,256]{2,1,0:T(8,128)(2,1)S(1)}, bf16[3,256,256]{2,1,0:T(8,128)(2,1)S(1)}) custom-call(s32[1]{0:T(128)} %bitcast.core_ref, bf16[1,256,256]{2,1,0:T(8,128)(2,1)} %keys_ref.1, bf16[1,256,256]{2,1,0:T(8,128)(2,1)} %values_ref.1, f32[1,256]{1,0:T(1,128)} %rate_ref.1, bf16[1,512,256]{2,1,0:T(8,128)(2,1)} %gate_ref.3, ...), custom_call_target="tpu_custom_call" | custom-call | flops 1048576 | bytes 1048576 | tf_op jit(solution)/shard_map/pallas_call | solution.py:262
  1.2 1.9 %collective-permute-start = (bf16[3,256,256]{2,1,0:T(8,128)(2,1)S(1)}, bf16[3,256,256]{2,1,0:T(8,128)(2,1)S(1)}, u32[]{:S(2)}, u32[]{:S(2)}) collective-permute-start(bf16[3,256,256]{2,1,0:T(8,128)(2,1)S(1)} %get-tuple-element.12.own_ref), channel_id=1, source_target_pairs={{0,4},{4,0},{1,5},{5,1},{2,6},{6,2},{3,7},{7,3},{8,12},{12,8},{9,1... | collective-permute-start | bytes 1179656 | tf_op jit(solution)/shard_map/ppermute | solution.py:48
  3.2 0.3 shard_map.92
  3.5 1.3 %collective-permute-done.partner_ref = bf16[3,256,256]{2,1,0:T(8,128)(2,1)S(1)} collective-permute-done((bf16[3,256,256]{2,1,0:T(8,128)(2,1)S(1)}, bf16[3,256,256]{2,1,0:T(8,128)(2,1)S(1)}, u32[]{:S(2)}, u32[]{:S(2)}) %collective-permute-start) | collective-permute-done | bytes 393248 | tf_op jit(solution)/shard_map/ppermute | solution.py:48
  4.9 0.7 shard_map.93
  5.5 20.9 %all_to_all.15 = bf16[16,16,768]{2,1,0:T(8,128)(2,1)S(1)} all-to-all(bf16[16,16,768]{2,1,0:T(8,128)(2,1)S(1)} %bitcast.6), channel_id=1, replica_groups={{256,264,272,280,384,392,400,408,0,8,16,24,128,136,144,152},{257,265,27..., dimensions={0} | all-to-all | bytes 786432 | tf_op jit(solution)/shard_map/all_to_all | solution.py:52
  26.5 0.1 reduce_sum.24
  26.6 18.3 %all_to_all.16 = bf16[4,16,768]{2,1,0:T(8,128)(2,1)S(1)} all-to-all(bf16[4,16,768]{2,1,0:T(8,128)(2,1)S(1)} %broadcast_in_dim.6), channel_id=1, replica_groups={{64,96,0,32},{65,97,1,33},{66,98,2,34},{67,99,3,35},{68,100,4,36},{69,1..., dimensions={0} | all-to-all | bytes 196608 | tf_op jit(solution)/shard_map/all_to_all | solution.py:52
  44.9 15.3 %all_to_all.17 = bf16[16,16,768]{2,1,0:T(8,128)(2,1)S(1)} all-to-all(bf16[16,16,768]{2,1,0:T(8,128)(2,1)S(1)} %broadcast_in_dim.7), channel_id=1, replica_groups={{256,264,272,280,384,392,400,408,0,8,16,24,128,136,144,152},{257,265,27..., dimensions={0} | all-to-all | bytes 786432 | tf_op jit(solution)/shard_map/all_to_all | solution.py:52
  60.2 1.9 %collective-permute-start.1 = (bf16[256,768]{1,0:T(8,128)(2,1)S(1)}, bf16[256,768]{1,0:T(8,128)(2,1)S(1)}, u32[]{:S(2)}, u32[]{:S(2)}) collective-permute-start(bf16[256,768]{1,0:T(8,128)(2,1)S(1)} %bitcast.4), channel_id=1, source_target_pairs={{0,4},{4,0},{1,5},{5,1},{2,6},{6,2},{3,7},{7,3},{8,12},{12,8},{9,1... | collective-permute-start | bytes 1179656 | tf_op jit(solution)/shard_map/ppermute | solution.py:48
  62.1 0.0 copy-start.3
  62.2 6.1 %collective-permute-start.2 = (bf16[2,128,256]{2,1,0:T(8,128)(2,1)S(1)}, bf16[2,128,256]{2,1,0:T(8,128)(2,1)S(1)}, u32[]{:S(2)}, u32[]{:S(2)}) collective-permute-start(bf16[2,128,256]{2,1,0:T(8,128)(2,1)S(1)} %maximum_select_fusion), channel_id=1, source_target_pairs={{4,8},{12,16},{20,24},{28,32},{36,40},{44,48},{52,56},{60,64},{68,... | collective-permute-start | bytes 393224 | tf_op jit(solution)/shard_map/ppermute | solution.py:44
  68.4 2.6 %collective-permute-done.2.outer_ref = bf16[2,128,256]{2,1,0:T(8,128)(2,1)S(1)} collective-permute-done((bf16[2,128,256]{2,1,0:T(8,128)(2,1)S(1)}, bf16[2,128,256]{2,1,0:T(8,128)(2,1)S(1)}, u32[]{:S(2)}, u32[]{:S(2)}) %collective-permute-start.2) | collective-permute-done | bytes 131104 | tf_op jit(solution)/shard_map/ppermute | solution.py:44
  71.0 0.0 copy-done.3
  71.0 0.0 copy-start
  71.0 0.0 copy-start.1
  71.0 0.0 copy-start.2
  71.0 1.3 %shard_map.95 = (f32[256,256]{1,0:T(8,128)S(1)}, f32[1,256]{1,0:T(1,128)S(1)}, f32[2,1,256]{2,1,0:T(1,128)S(1)}) custom-call(s32[1]{0:T(128)} %bitcast.core_ref, s32[1]{0:T(128)} %bitcast.3.has_outer_ref, bf16[1,256,256]{2,1,0:T(8,128)(2,1)S(1)} %copy-done.3, bf16[3,256,256]{2,1,0:T(8,128)(2,1)S(1)} %get-tuple-element.12.own_ref, ...), custom_call_target="tpu_custom_call" | custom-call | flops 268435456 | bytes 1048576 | tf_op jit(solution)/shard_map/pallas_call | solution.py:262
  72.3 2.7 %collective-permute-start.3 = (f32[1,256]{1,0:T(1,128)S(1)}, f32[1,256]{1,0:T(1,128)S(1)}, u32[]{:S(2)}, u32[]{:S(2)}) collective-permute-start(f32[1,256]{1,0:T(1,128)S(1)} %get-tuple-element.17), channel_id=1, source_target_pairs={{0,1},{1,0},{2,3},{3,2},{4,5},{5,4},{6,7},{7,6},{8,9},{9,8},{10,11... | collective-permute-start | bytes 3080 | tf_op jit(solution)/shard_map/ppermute | solution.py:67
  75.0 2.7 %collective-permute-done.3 = f32[1,256]{1,0:T(1,128)S(1)} collective-permute-done((f32[1,256]{1,0:T(1,128)S(1)}, f32[1,256]{1,0:T(1,128)S(1)}, u32[]{:S(2)}, u32[]{:S(2)}) %collective-permute-start.3) | collective-permute-done | bytes 1056 | tf_op jit(solution)/shard_map/ppermute | solution.py:67
  77.8 2.4 %collective-permute-start.4 = (f32[1,256]{1,0:T(1,128)S(1)}, f32[1,256]{1,0:T(1,128)S(1)}, u32[]{:S(2)}, u32[]{:S(2)}) collective-permute-start(f32[1,256]{1,0:T(1,128)S(1)} %add.18), channel_id=1, source_target_pairs={{0,3},{1,2},{2,1},{3,0},{4,7},{5,6},{6,5},{7,4},{8,11},{9,10},{10,... | collective-permute-start | bytes 3080 | tf_op jit(solution)/shard_map/ppermute | solution.py:67
  80.1 0.0 copy-done
  80.2 0.0 copy-done.1
  80.2 0.0 copy-done.2
  80.2 0.3 shard_map.94.turned_ref
  80.4 4.0 %collective-permute-done.4 = f32[1,256]{1,0:T(1,128)S(1)} collective-permute-done((f32[1,256]{1,0:T(1,128)S(1)}, f32[1,256]{1,0:T(1,128)S(1)}, u32[]{:S(2)}, u32[]{:S(2)}) %collective-permute-start.4) | collective-permute-done | bytes 1056 | tf_op jit(solution)/shard_map/ppermute | solution.py:67
  84.4 0.0 collective-permute-done.1.partner_ref
  84.4 2.8 %shard_map.96 = bf16[1,256,256]{2,1,0:T(8,128)(2,1)} custom-call(bf16[256,768]{1,0:T(8,128)(2,1)S(1)} %bitcast.5, bf16[256,768]{1,0:T(8,128)(2,1)S(1)} %collective-permute-done.1.partner_ref, bf16[3,256,512]{2,1,0:T(8,128)(2,1)S(1)} %shard_map.94.turned_ref, bf16[1,256,256]{2,1,0:T(8,128)(2,1)S(1)} %copy-done.3, ...), custom_call_target="tpu_custom_call" | custom-call | flops 3221225472 | bytes 1048576 | tf_op jit(solution)/shard_map/pallas_call | solution.py:262
  (7 shorter events, 0.1 us)
Async XLA Ops:
  1.2 3.6 %collective-permute-start = (bf16[3,256,256]{2,1,0:T(8,128)(2,1)S(1)}, bf16[3,256,256]{2,1,0:T(8,128)(2,1)S(1)}, u32[]{:S(2)}, u32[]{:S(2)}) collective-permute-start(bf16[3,256,256]{2,1,0:T(8,128)(2,1)S(1)} %get-tuple-element.12.own_ref), channel_id=1, source_target_pairs={{0,4},{4,0},{1,5},{5,1},{2,6},{6,2},{3,7},{7,3},{8,12},{12,8},{9,1... | collective-permute-start | bytes 1179656 | tf_op jit(solution)/shard_map/ppermute | solution.py:48
  60.2 24.2 %collective-permute-start.1 = (bf16[256,768]{1,0:T(8,128)(2,1)S(1)}, bf16[256,768]{1,0:T(8,128)(2,1)S(1)}, u32[]{:S(2)}, u32[]{:S(2)}) collective-permute-start(bf16[256,768]{1,0:T(8,128)(2,1)S(1)} %bitcast.4), channel_id=1, source_target_pairs={{0,4},{4,0},{1,5},{5,1},{2,6},{6,2},{3,7},{7,3},{8,12},{12,8},{9,1... | collective-permute-start | bytes 1179656 | tf_op jit(solution)/shard_map/ppermute | solution.py:48
  62.1 8.8 %copy-start.3 = (bf16[1,256,256]{2,1,0:T(8,128)(2,1)S(1)}, bf16[1,256,256]{2,1,0:T(8,128)(2,1)}, u32[]{:S(2)}) copy-start(bf16[1,256,256]{2,1,0:T(8,128)(2,1)} %queries_ref.3) | copy-start | bytes 393220
  62.2 8.8 %collective-permute-start.2 = (bf16[2,128,256]{2,1,0:T(8,128)(2,1)S(1)}, bf16[2,128,256]{2,1,0:T(8,128)(2,1)S(1)}, u32[]{:S(2)}, u32[]{:S(2)}) collective-permute-start(bf16[2,128,256]{2,1,0:T(8,128)(2,1)S(1)} %maximum_select_fusion), channel_id=1, source_target_pairs={{4,8},{12,16},{20,24},{28,32},{36,40},{44,48},{52,56},{60,64},{68,... | collective-permute-start | bytes 393224 | tf_op jit(solution)/shard_map/ppermute | solution.py:44
  71.0 9.2 %copy-start = (bf16[1,512,256]{2,1,0:T(8,128)(2,1)S(1)}, bf16[1,512,256]{2,1,0:T(8,128)(2,1)}, u32[]{:S(2)}) copy-start(bf16[1,512,256]{2,1,0:T(8,128)(2,1)} %gate_ref.3) | copy-start | bytes 786436
  71.0 9.2 %copy-start.1 = (bf16[1,512,256]{2,1,0:T(8,128)(2,1)S(1)}, bf16[1,512,256]{2,1,0:T(8,128)(2,1)}, u32[]{:S(2)}) copy-start(bf16[1,512,256]{2,1,0:T(8,128)(2,1)} %up_ref.3) | copy-start | bytes 786436
  71.0 9.2 %copy-start.2 = (bf16[1,512,256]{2,1,0:T(8,128)(2,1)S(1)}, bf16[1,512,256]{2,1,0:T(8,128)(2,1)}, u32[]{:S(2)}) copy-start(bf16[1,512,256]{2,1,0:T(8,128)(2,1)} %down_ref.3) | copy-start | bytes 786436
  72.3 5.5 %collective-permute-start.3 = (f32[1,256]{1,0:T(1,128)S(1)}, f32[1,256]{1,0:T(1,128)S(1)}, u32[]{:S(2)}, u32[]{:S(2)}) collective-permute-start(f32[1,256]{1,0:T(1,128)S(1)} %get-tuple-element.17), channel_id=1, source_target_pairs={{0,1},{1,0},{2,3},{3,2},{4,5},{5,4},{6,7},{7,6},{8,9},{9,8},{10,11... | collective-permute-start | bytes 3080 | tf_op jit(solution)/shard_map/ppermute | solution.py:67
  77.8 6.7 %collective-permute-start.4 = (f32[1,256]{1,0:T(1,128)S(1)}, f32[1,256]{1,0:T(1,128)S(1)}, u32[]{:S(2)}, u32[]{:S(2)}) collective-permute-start(f32[1,256]{1,0:T(1,128)S(1)} %add.18), channel_id=1, source_target_pairs={{0,3},{1,2},{2,1},{3,0},{4,7},{5,6},{6,5},{7,4},{8,11},{9,10},{10,... | collective-permute-start | bytes 3080 | tf_op jit(solution)/shard_map/ppermute | solution.py:67
